TPU v7x, 32 devices: a whole 2x2x4 slice. The times are simulated.
32 devices in a mesh: fsdp: 2 (over x), ctx: 4 (over y, core), tp: 4 (over z).
Axes of the slice: x: 2, y: 2, z: 4, core: 2. Of those that a mesh axis runs over, the one named last changes fastest.
Arguments:
- inputs: bfloat16 [8, 2048, 768], P('fsdp', ('ctx', 'tp')), may hold values from -6 to 6
- segments: int32 [8, 2048], P('fsdp'), may hold values from 0 to 15, never falling along the last dimension, each value on 1 to 1024 neighbouring positions
- query_weight: bfloat16 [768, 768], P(('fsdp', 'ctx'), 'tp'), may hold values from -0.3125 to 0.3125
- query_bias: float32 [768], P('tp'), may hold values from -1.5 to 1.5
- key_weight: bfloat16 [768, 768], P(('fsdp', 'ctx'), 'tp'), may hold values from -0.3125 to 0.3125
- value_weight: bfloat16 [768, 768], P(('fsdp', 'ctx'), 'tp'), may hold values from -0.21875 to 0.21875
- value_bias: float32 [768], P('tp'), may hold values from -1.5 to 1.5
- output_weight: bfloat16 [768, 768], P('tp', ('fsdp', 'ctx')), may hold values from -1.25 to 1.25
- output_bias: float32 [768], replicated, may hold values from -1.5 to 1.5
- first_gain: float32 [768], replicated, may hold values from 0.5 to 1.5
- first_shift: float32 [768], replicated, may hold values from -1.5 to 1.5
- expand_weight: bfloat16 [768, 3072], P(('fsdp', 'ctx'), 'tp'), may hold values from -0.21875 to 0.21875
- expand_bias: float32 [3072], P('tp'), may hold values from -1.5 to 1.5
- contract_weight: bfloat16 [3072, 768], P('tp', ('fsdp', 'ctx')), may hold values from -0.15625 to 0.15625
- contract_bias: float32 [768], replicated, may hold values from -1.5 to 1.5
- second_gain: float32 [768], replicated, may hold values from 0.5 to 1.5
- second_shift: float32 [768], replicated, may hold values from -1.5 to 1.5
- cotangent: bfloat16 [8, 2048, 768], P('fsdp', ('ctx', 'tp')), may hold values from -6 to 6
Outputs:
- outputs: bfloat16 [8, 2048, 768], P('fsdp', ('ctx', 'tp'))
- input_grad: bfloat16 [8, 2048, 768], P('fsdp', ('ctx', 'tp'))
- query_weight_grad: float32 [768, 768], P(('fsdp', 'ctx'), 'tp')
- query_bias_grad: float32 [768], P('tp')
- key_weight_grad: float32 [768, 768], P(('fsdp', 'ctx'), 'tp')
- value_weight_grad: float32 [768, 768], P(('fsdp', 'ctx'), 'tp')
- value_bias_grad: float32 [768], P('tp')
- output_weight_grad: float32 [768, 768], P('tp', ('fsdp', 'ctx'))
- output_bias_grad: float32 [768], replicated
- first_gain_grad: float32 [768], replicated
- first_shift_grad: float32 [768], replicated
- expand_weight_grad: float32 [768, 3072], P(('fsdp', 'ctx'), 'tp')
- expand_bias_grad: float32 [3072], P('tp')
- contract_weight_grad: float32 [3072, 768], P('tp', ('fsdp', 'ctx'))
- contract_bias_grad: float32 [768], replicated
- second_gain_grad: float32 [768], replicated
- second_shift_grad: float32 [768], replicated
Inputs may be any that keep to these rules, and one draw needn't show every extreme that they name: `segments`: along each sequence the segment numbers never fall and take every value 0 to 15; a document has at most 1024 tokens, and one document of each sequence has exactly 1024.
All inputs are finite; a program needn't handle non-finite values.
Results may differ from a plain program's by a relative error of at most 0.022.
Values may be sent and summed in bfloat16 or wider, within the bound.
No kernel may reach another device: no remote copies, remote signals or barrier semaphores. Data moves between devices by JAX's collectives and lax.ppermute only.
A program may use at most 192 MiB of HBM per device.

v0:
```python
import jax
import jax.numpy as jnp
from jax import lax
from jax.sharding import PartitionSpec as P

HEAD_DIM = 64


epsilon = 1e-05
masked_value = -1e30


def in_blocks(value, dim, count):
    lengths = value.shape
    tiles = value.reshape(*lengths[:dim], count, lengths[dim] // count, *lengths[dim + 1 :])
    return jnp.moveaxis(tiles, dim, 0)


def sent_and_summed(value, axis, dim):
    count = lax.axis_size(axis)
    tiles = lax.all_to_all(in_blocks(value, dim, count), axis, 0, 0, tiled=True)
    return jnp.sum(tiles.astype(jnp.float32), axis=0)


def in_one_piece(arrays, axis, dim, along):
    both = jnp.concatenate(arrays, axis=along)
    out, at, done = (sent_and_summed(both, axis, dim), 0, [])
    for a in arrays:
        done.append(lax.slice_in_dim(out, at, at + a.shape[along], axis=along))
        at += a.shape[along]
    return tuple(done)


def exact_gelu(values):
    return jax.nn.gelu(values, approximate=False)


def whole_rows(tensor):
    return lax.all_gather(tensor, "tp", axis=1, tiled=True)


def feature_sum(tensor):
    return lax.psum_scatter(
        tensor.astype(jnp.bfloat16), "tp", scatter_dimension=1, tiled=True
    ).astype(jnp.float32)


def fetch_weights(
    query_weight, key_weight, value_weight, expand_weight, output_weight, contract_weight
):
    front_set = (
        lax.all_gather(query_weight, ("fsdp", "ctx"), axis=0, tiled=True),
        lax.all_gather(key_weight, ("fsdp", "ctx"), axis=0, tiled=True),
        lax.all_gather(value_weight, ("fsdp", "ctx"), axis=0, tiled=True),
        lax.all_gather(expand_weight, ("fsdp", "ctx"), axis=0, tiled=True),
    )
    back_set = (
        lax.all_gather(output_weight, ("fsdp", "ctx"), axis=1, tiled=True),
        lax.all_gather(contract_weight, ("fsdp", "ctx"), axis=1, tiled=True),
    )
    return (front_set, back_set)


def fetch_blocks(keys_low, values_low):
    return (
        lax.all_gather(keys_low, "ctx", axis=1, tiled=True),
        lax.all_gather(values_low, "ctx", axis=1, tiled=True),
    )


def to_items(tensor):
    seq_count, row_count, feat_count = tensor.shape
    heads_here = feat_count // HEAD_DIM
    shaped = tensor.reshape(seq_count, row_count, heads_here, HEAD_DIM).transpose(0, 2, 1, 3)
    return shaped.reshape(seq_count * heads_here, row_count, HEAD_DIM)


def from_items(tensor, seq_count):
    item_count, row_count, _ = tensor.shape
    heads_here = item_count // seq_count
    shaped = tensor.reshape(seq_count, heads_here, row_count, HEAD_DIM).transpose(0, 2, 1, 3)
    return shaped.reshape(seq_count, row_count, heads_here * HEAD_DIM)


def masked_scores(query_rows, key_rows, query_segs, key_segs):
    raw_scores = lax.dot_general(
        query_rows, key_rows, (((1,), (1,)), ((), ())), preferred_element_type=jnp.float32
    ) * HEAD_DIM ** (-0.5)
    return jnp.where(query_segs[:, None] == key_segs[None, :], raw_scores, masked_value)


def attend(pieces):
    query_rows, key_rows, value_rows, query_segs, key_segs = pieces
    scores = masked_scores(query_rows, key_rows, query_segs, key_segs)
    highest = jnp.max(scores, axis=1, keepdims=True)
    weights = jnp.exp(scores - highest)
    totals = jnp.sum(weights, axis=1, keepdims=True)
    softmax_rows = (weights / totals).astype(jnp.bfloat16)
    attended = jnp.dot(softmax_rows, value_rows, preferred_element_type=jnp.float32)
    return (attended, (highest + jnp.log(totals))[:, 0])


def attend_back(pieces):
    query_rows, key_rows, value_rows, grad_rows, log_totals, deltas, query_segs, key_segs = pieces
    scores = masked_scores(query_rows, key_rows, query_segs, key_segs)
    softmax_rows = jnp.exp(scores - log_totals[:, None])
    grad_softmax = lax.dot_general(
        grad_rows, value_rows, (((1,), (1,)), ((), ())), preferred_element_type=jnp.float32
    )
    grad_scores = (softmax_rows * (grad_softmax - deltas[:, None])).astype(jnp.bfloat16)
    score_scale = HEAD_DIM ** (-0.5)
    grad_query = jnp.dot(grad_scores, key_rows, preferred_element_type=jnp.float32) * score_scale
    grad_keys = (
        lax.dot_general(
            grad_scores, query_rows, (((0,), (0,)), ((), ())), preferred_element_type=jnp.float32
        )
        * score_scale
    )
    grad_values = lax.dot_general(
        softmax_rows.astype(jnp.bfloat16),
        grad_rows,
        (((0,), (0,)), ((), ())),
        preferred_element_type=jnp.float32,
    )
    return (grad_query, grad_keys, grad_values)


def norm_forward(resid, gain, shift):
    row_mean = jnp.mean(resid, axis=2, keepdims=True)
    spread = jnp.mean(resid * resid, axis=2, keepdims=True) - row_mean * row_mean
    inverse = lax.rsqrt(spread + epsilon)
    normed = (resid - row_mean) * inverse
    return (normed * gain + shift, normed, inverse)


def norm_backward(upstream, normed, inverse, gain):
    scaled = upstream * gain
    first_mean = jnp.mean(scaled, axis=2, keepdims=True)
    second_mean = jnp.mean(scaled * normed, axis=2, keepdims=True)
    back_term = inverse * (scaled - first_mean - normed * second_mean)
    return (back_term, jnp.sum(upstream * normed, axis=(0, 1)), jnp.sum(upstream, axis=(0, 1)))


def token_sum(tensor):
    return jnp.sum(tensor.astype(jnp.float32), axis=(0, 1))


def per_device(
    inputs,
    segments,
    query_weight,
    query_bias,
    key_weight,
    value_weight,
    value_bias,
    output_weight,
    output_bias,
    first_gain,
    first_shift,
    expand_weight,
    expand_bias,
    contract_weight,
    contract_bias,
    second_gain,
    second_shift,
    cotangent,
):
    seq_count, rows_here, _ = inputs.shape
    ctx_rows = rows_here * lax.axis_size("tp")
    heads_here = query_weight.shape[1] // HEAD_DIM
    own_segments = lax.dynamic_slice_in_dim(segments, lax.axis_index("ctx") * ctx_rows, ctx_rows, 1)
    query_segs = jnp.repeat(own_segments, heads_here, axis=0)
    key_segs = jnp.repeat(segments, heads_here, axis=0)
    front_set, back_set = fetch_weights(
        query_weight, key_weight, value_weight, expand_weight, output_weight, contract_weight
    )
    query_full, key_full, value_full, expand_full = front_set
    output_full, contract_full = back_set
    inputs_whole = whole_rows(inputs)
    query_low = (
        jnp.einsum("scd,de->sce", inputs_whole, query_full, preferred_element_type=jnp.float32)
        + query_bias
    ).astype(jnp.bfloat16)
    keys_low = jnp.einsum(
        "scd,de->sce", inputs_whole, key_full, preferred_element_type=jnp.float32
    ).astype(jnp.bfloat16)
    values_low = (
        jnp.einsum("scd,de->sce", inputs_whole, value_full, preferred_element_type=jnp.float32)
        + value_bias
    ).astype(jnp.bfloat16)
    keys_all, values_all = fetch_blocks(keys_low, values_low)
    query_items = to_items(query_low)
    attended_items, log_totals = lax.map(
        attend, (query_items, to_items(keys_all), to_items(values_all), query_segs, key_segs)
    )
    attended = from_items(attended_items, seq_count)
    attended_low = attended.astype(jnp.bfloat16)
    branch = (
        feature_sum(
            jnp.einsum("sce,ed->scd", attended_low, output_full, preferred_element_type=jnp.float32)
        )
        + output_bias
    )
    middle, middle_normed, middle_inverse = norm_forward(
        inputs.astype(jnp.float32) + branch, first_gain, first_shift
    )
    middle_whole = whole_rows(middle.astype(jnp.bfloat16))
    preact = (
        jnp.einsum("scd,df->scf", middle_whole, expand_full, preferred_element_type=jnp.float32)
        + expand_bias
    )
    active, gelu_pull = jax.vjp(exact_gelu, preact)
    active_low = active.astype(jnp.bfloat16)
    feedforward = (
        feature_sum(
            jnp.einsum("scf,fd->scd", active_low, contract_full, preferred_element_type=jnp.float32)
        )
        + contract_bias
    )
    outputs, final_normed, final_inverse = norm_forward(
        middle + feedforward, second_gain, second_shift
    )
    front_use, back_use = fetch_weights(
        query_weight, key_weight, value_weight, expand_weight, output_weight, contract_weight
    )
    keys_use, values_use = fetch_blocks(keys_low, values_low)
    query_use, key_use, value_use, expand_use = front_use
    output_use, contract_use = back_use
    final_grad, second_gain_grad, second_shift_grad = norm_backward(
        cotangent.astype(jnp.float32), final_normed, final_inverse, second_gain
    )
    feed_grad = final_grad.astype(jnp.bfloat16)
    contract_bias_grad = token_sum(feed_grad)
    feed_whole = whole_rows(feed_grad)
    contract_part = jnp.einsum(
        "scf,scd->fd", active_low, feed_whole, preferred_element_type=jnp.float32
    )
    active_grad = jnp.einsum(
        "scd,fd->scf", feed_whole, contract_use, preferred_element_type=jnp.float32
    )
    preact_grad = gelu_pull(active_grad)[0].astype(jnp.bfloat16)
    expand_bias_grad = token_sum(preact_grad)
    expand_part = jnp.einsum(
        "scd,scf->df", middle_whole, preact_grad, preferred_element_type=jnp.float32
    )
    middle_grad = final_grad + feature_sum(
        jnp.einsum("scf,df->scd", preact_grad, expand_use, preferred_element_type=jnp.float32)
    )
    resid_grad, first_gain_grad, first_shift_grad = norm_backward(
        middle_grad, middle_normed, middle_inverse, first_gain
    )
    branch_grad = resid_grad.astype(jnp.bfloat16)
    output_bias_grad = token_sum(branch_grad)
    branch_whole = whole_rows(branch_grad)
    output_part = jnp.einsum(
        "sce,scd->ed", attended_low, branch_whole, preferred_element_type=jnp.float32
    )
    attended_grad = jnp.einsum(
        "scd,ed->sce", branch_whole, output_use, preferred_element_type=jnp.float32
    ).astype(jnp.bfloat16)
    deltas = jnp.sum(
        (attended_grad.astype(jnp.float32) * attended).reshape(
            seq_count, ctx_rows, heads_here, HEAD_DIM
        ),
        axis=3,
    ).transpose(0, 2, 1)
    delta_items = deltas.reshape(seq_count * heads_here, ctx_rows)
    grad_items = to_items(attended_grad)
    query_back, keys_part, values_part = lax.map(
        attend_back,
        (
            query_items,
            to_items(keys_use),
            to_items(values_use),
            grad_items,
            log_totals,
            delta_items,
            query_segs,
            key_segs,
        ),
    )
    keys_grad, values_grad = (
        lax.psum_scatter(
            from_items(keys_part, seq_count).astype(jnp.bfloat16),
            "ctx",
            scatter_dimension=1,
            tiled=True,
        ).astype(jnp.float32),
        lax.psum_scatter(
            from_items(values_part, seq_count).astype(jnp.bfloat16),
            "ctx",
            scatter_dimension=1,
            tiled=True,
        ).astype(jnp.float32),
    )
    query_grad = from_items(query_back, seq_count).astype(jnp.bfloat16)
    keys_grad_low = keys_grad.astype(jnp.bfloat16)
    values_grad_low = values_grad.astype(jnp.bfloat16)
    query_bias_grad = token_sum(query_grad)
    value_bias_grad = token_sum(values_grad_low)
    query_part = jnp.einsum(
        "scd,sce->de", inputs_whole, query_grad, preferred_element_type=jnp.float32
    )
    key_part = jnp.einsum(
        "scd,sce->de", inputs_whole, keys_grad_low, preferred_element_type=jnp.float32
    )
    value_part = jnp.einsum(
        "scd,sce->de", inputs_whole, values_grad_low, preferred_element_type=jnp.float32
    )
    input_terms = (
        jnp.einsum("sce,de->scd", query_grad, query_use, preferred_element_type=jnp.float32)
        + jnp.einsum("sce,de->scd", keys_grad_low, key_use, preferred_element_type=jnp.float32)
        + jnp.einsum("sce,de->scd", values_grad_low, value_use, preferred_element_type=jnp.float32)
    )
    input_grad = (resid_grad + feature_sum(input_terms)).astype(jnp.bfloat16)
    query_weight_grad, key_weight_grad, value_weight_grad, expand_weight_grad = in_one_piece(
        (
            query_part.astype(jnp.bfloat16),
            key_part.astype(jnp.bfloat16),
            value_part.astype(jnp.bfloat16),
            expand_part.astype(jnp.bfloat16),
        ),
        ("fsdp", "ctx"),
        0,
        1,
    )
    output_weight_grad, contract_weight_grad = in_one_piece(
        (output_part.astype(jnp.bfloat16), contract_part.astype(jnp.bfloat16)),
        ("fsdp", "ctx"),
        1,
        0,
    )
    column_sums = lax.psum((query_bias_grad, value_bias_grad, expand_bias_grad), ("fsdp", "ctx"))
    whole_sums = lax.psum(
        (
            output_bias_grad,
            first_gain_grad,
            first_shift_grad,
            contract_bias_grad,
            second_gain_grad,
            second_shift_grad,
        ),
        ("fsdp", "ctx", "tp"),
    )
    return (
        outputs.astype(jnp.bfloat16),
        input_grad,
        query_weight_grad,
        column_sums[0],
        key_weight_grad,
        value_weight_grad,
        column_sums[1],
        output_weight_grad,
        whole_sums[0],
        whole_sums[1],
        whole_sums[2],
        expand_weight_grad,
        column_sums[2],
        contract_weight_grad,
        whole_sums[3],
        whole_sums[4],
        whole_sums[5],
    )


def solution(mesh):
    placed = (
        P("fsdp", ("ctx", "tp"), None),
        P("fsdp", None),
        P(("fsdp", "ctx"), "tp"),
        P("tp"),
        P(("fsdp", "ctx"), "tp"),
        P(("fsdp", "ctx"), "tp"),
        P("tp"),
        P("tp", ("fsdp", "ctx")),
        P(),
        P(),
        P(),
        P(("fsdp", "ctx"), "tp"),
        P("tp"),
        P("tp", ("fsdp", "ctx")),
        P(),
        P(),
        P(),
        P("fsdp", ("ctx", "tp"), None),
    )
    return jax.shard_map(
        per_device,
        mesh=mesh,
        in_specs=placed,
        out_specs=(
            P("fsdp", ("ctx", "tp"), None),
            P("fsdp", ("ctx", "tp"), None),
            P(("fsdp", "ctx"), "tp"),
            P("tp"),
            P(("fsdp", "ctx"), "tp"),
            P(("fsdp", "ctx"), "tp"),
            P("tp"),
            P("tp", ("fsdp", "ctx")),
            P(),
            P(),
            P(),
            P(("fsdp", "ctx"), "tp"),
            P("tp"),
            P("tp", ("fsdp", "ctx")),
            P(),
            P(),
            P(),
        ),
        check_vma=False,
    )
```

profile of v0, /device:TPU:0, one launch (start us, length us, event | category | flops | bytes accessed | tf_op | source)
XLA Modules:
  0.0 1107.4 jit_solution(9086204547020164236)
XLA Ops:
  8.8 11.3 %all_gather.48 = bf16[768,192]{1,0:T(8,128)(2,1)S(1)} all-gather(bf16[96,192]{1,0:T(8,128)(2,1)} %param.27), channel_id=1, replica_groups=mesh['fsdp'=2,'ctx'=4,'tp'=4] {'fsdp','ctx'}, dimensions={0}, use_global_device_ids=true | all-gather | bytes 331776 | tf_op jit(solution)/shard_map/all_gather | solution.py:54
  20.1 56.5 %all-gather.9.cloned.1.call-done = bf16[4,512,768]{2,1,0:T(8,128)(2,1)} async-done(((bf16[4,128,768]{2,1,0:T(8,128)(2,1)}), bf16[4,512,768]{2,1,0:T(8,128)(2,1)}) %all-gather.9.cloned.1.call-update) | async-done | bytes 3145744 | tf_op jit(solution)/shard_map/all_gather | solution.py:39
  76.6 4.1 add_convert_fusion.4
  80.8 9.9 all_gather.46
  100.1 10.6 all_gather.45
  110.7 10.4 all_gather.50
  126.6 4.5 copy.103
  131.2 9.1 all-gather.11.cloned.1.call-done
  142.9 4.5 copy.102
  147.4 137.5 %while.28 = (s32[]{:T(128)}, f32[12,512,64]{1,2,0:T(8,128)}, f32[12,512]{1,0:T(8,128)}, s32[12,512]{1,0:T(8,128)}, s32[12,2048]{1,0:T(8,128)}, /*index=5*/bf16[1...) while((s32[]{:T(128)}, f32[12,512,64]{1,2,0:T(8,128)}, ...), condition=%wide.region_3.4_spmd.clone, body=%wide.region_0.3_spmd.sunk.clone | while | flops 277872128 | bytes 30724220 | solution.py:193
  155.0 3.9 fusion.151
  166.5 3.9 fusion.151
  177.9 3.9 fusion.151
  189.4 3.9 fusion.151
  200.8 3.9 fusion.151
  212.3 3.9 fusion.151
  223.7 3.9 fusion.151
  235.2 3.9 fusion.151
  246.7 3.9 fusion.151
  258.1 3.9 fusion.151
  269.6 3.9 fusion.151
  281.0 3.9 fusion.151
  290.3 59.4 %reduce-scatter.7.cloned.1.call-done = bf16[4,128,768]{2,1,0:T(8,128)(2,1)} async-done(((bf16[4,512,768]{2,1,0:T(8,128)(2,1)}), bf16[4,128,768]{2,1,0:T(8,128)(2,1)}) %reduce-scatter.7.cloned.1.call-update) | async-done | bytes 786448 | tf_op jit(solution)/shard_map/reduce_scatter | solution.py:43
  354.6 62.7 %all-gather.15.cloned.1.call-done = bf16[4,512,768]{2,1,0:T(8,128)(2,1)} async-done(((bf16[4,128,768]{2,1,0:T(8,128)(2,1)}), bf16[4,512,768]{2,1,0:T(8,128)(2,1)}) %all-gather.15.cloned.1.call-update) | async-done | bytes 3145744 | tf_op jit(solution)/shard_map/all_gather | solution.py:39
  417.2 6.4 fusion.51
  426.3 15.6 %multiply_convert_fusion.1 = (bf16[4,512,768]{2,1,0:T(8,128)(2,1)}, f32[4,512,768]{2,1,0:T(8,128)}) fusion(f32[4,512,768]{2,1,0:T(8,128)S(1)} %get-tuple-element.315, f32[768]{0:T(1024)S(1)} %copy-done.37, u8[512,768]{1,0:T(8,128)(4,1)S(1)} %get-tuple-element.221, u8[512,768]{1,0:T(8,128)(4,1)S(1)} %get-tuple-element.220), kind=kLoop, calls=%fused_computation.62 | loop fusion | flops 111673344 | bytes 16518144 | tf_op jit(solution)/shard_map/convert_element_type | solution.py:213
  441.8 6.6 convolution_convert_fusion.2
  448.5 60.1 %reduce-scatter.9.cloned.1.call-done = bf16[4,128,768]{2,1,0:T(8,128)(2,1)} async-done(((bf16[4,512,768]{2,1,0:T(8,128)(2,1)}), bf16[4,128,768]{2,1,0:T(8,128)(2,1)}) %reduce-scatter.9.cloned.1.call-update) | async-done | bytes 786448 | tf_op jit(solution)/shard_map/reduce_scatter | solution.py:43
  516.5 63.1 %all-gather.21.cloned.1.call-done = bf16[4,512,768]{2,1,0:T(8,128)(2,1)} async-done(((bf16[4,128,768]{2,1,0:T(8,128)(2,1)}), bf16[4,512,768]{2,1,0:T(8,128)(2,1)}) %all-gather.21.cloned.1.call-update) | async-done | bytes 3145744 | tf_op jit(solution)/shard_map/all_gather | solution.py:39
  579.6 11.1 %convert_reduce_fusion = (f32[768]{0:T(1024)}, bf16[4,512,768]{2,1,0:T(8,128)(2,1)S(1)}) fusion(f32[4,512,768]{2,1,0:T(8,128)} %get-tuple-element.290, bf16[4,512,768]{2,1,0:T(8,128)(2,1)} %all-gather.21.cloned.1.call-done, bf16[768,768]{0,1:T(8,128)(2,1)} %all-gather.19.cloned.1.call-done, f32[4,512,768]{2,1,0:T(8,128)} %copy-done.5, f32[768]{0:T(1024)} %param.34), kind=kOutput, calls=%fused_computation.59 | convolution fusion | flops 2442657024 | bytes 20060160 | tf_op jit(solution)/shard_map/scd,fd->scf/dot_general | solution.py:238
  592.3 4.0 convolution_convert_fusion.1
  596.4 59.1 %reduce-scatter.11.cloned.1.call-done = bf16[4,128,768]{2,1,0:T(8,128)(2,1)} async-done(((bf16[4,512,768]{2,1,0:T(8,128)(2,1)}), bf16[4,128,768]{2,1,0:T(8,128)(2,1)}) %reduce-scatter.11.cloned.1.call-update) | async-done | bytes 786448 | tf_op jit(solution)/shard_map/reduce_scatter | solution.py:43
  655.5 4.2 multiply_reduce_fusion
  663.2 63.3 %all-gather.23.cloned.1.call-done = bf16[4,512,768]{2,1,0:T(8,128)(2,1)} async-done(((bf16[4,128,768]{2,1,0:T(8,128)(2,1)}), bf16[4,512,768]{2,1,0:T(8,128)(2,1)}) %all-gather.23.cloned.1.call-update) | async-done | bytes 3145744 | tf_op jit(solution)/shard_map/all_gather | solution.py:39
  726.5 3.2 convolution_convert_fusion.3
  737.0 149.8 %while.29 = (s32[]{:T(128)}, bf16[12,512,64]{1,2,0:T(8,128)(2,1)S(1)}, bf16[12,2048,64]{1,2,0:T(8,128)(2,1)}, bf16[12,2048,64]{1,2,0:T(8,128)(2,1)}, s32[12,512]...) while((s32[]{:T(128)}, ...), condition=%wide.region_17.18_spmd.clone, body=%wide.region_16.17_spmd.sunk.clone | while | flops 679641088 | bytes 22199424 | solution.py:269
  887.9 3.7 fusion.74
  891.6 31.8 %reduce-scatter.13.cloned.1.call-done = bf16[4,512,192]{1,2,0:T(8,128)(2,1)} async-done(((bf16[4,2048,192]{1,2,0:T(8,128)(2,1)}), bf16[4,512,192]{1,2,0:T(8,128)(2,1)}) %reduce-scatter.13.cloned.1.call-update) | async-done | bytes 786448 | tf_op jit(solution)/shard_map/reduce_scatter | solution.py:283
  923.4 4.8 fusion.71
  928.3 35.4 %reduce-scatter.15.cloned.1.call-done = bf16[4,512,192]{1,2,0:T(8,128)(2,1)} async-done(((bf16[4,2048,192]{1,2,0:T(8,128)(2,1)}), bf16[4,512,192]{1,2,0:T(8,128)(2,1)}) %reduce-scatter.15.cloned.1.call-update) | async-done | bytes 786448 | tf_op jit(solution)/shard_map/reduce_scatter | solution.py:289
  963.7 7.6 add_convert_fusion
  971.3 5.7 bitcast_convert_fusion
  984.4 4.3 all-to-all-start.1
  995.2 4.1 copy.84
  999.4 9.4 all-to-all-done.1
  1008.8 4.4 all-to-all-start
  1013.2 60.9 %all-reduce = (f32[768]{0:T(1024)}, f32[768]{0:T(1024)}, f32[768]{0:T(1024)}, f32[768]{0:T(1024)}, f32[768]{0:T(1024)}, /*index=5*/f32[768]{0:T(1024)}) all-reduce(f32[768]{0:T(1024)S(1)} %copy-done.35, f32[768]{0:T(1024)S(1)} %copy-done.33, f32[768]{0:T(1024)S(1)} %copy-done.34, ...), channel_id=1, replica_groups=mesh['fsdp'=2,'ctx'=4,'tp'=4] {'fsdp','ctx','tp'}, use_global_device_ids=true, to_apply=%region_29.30 | all-reduce | flops 4608 | bytes 36864 | tf_op jit(solution)/shard_map/psum | solution.py:334
  1079.2 13.9 %all-reduce.1 = (f32[192]{0:T(256)}, f32[192]{0:T(256)}, f32[768]{0:T(1024)}) all-reduce(f32[192]{0:T(256)S(1)} %reduce_sum.211, f32[192]{0:T(256)S(1)} %convert_reduce_fusion.6, f32[768]{0:T(1024)S(1)} %copy-done.38), channel_id=1, replica_groups=mesh['fsdp'=2,'ctx'=4,'tp'=4] {'fsdp','ctx'}, use_global_device_ids=true, to_apply=%region_24.25 | all-reduce | flops 1152 | bytes 9216 | tf_op jit(solution)/shard_map/psum | solution.py:333
  (371 shorter events, 317.3 us)
Async XLA Ops:
  8.0 68.6 %all-gather.9.cloned.1.call-start = ((), (), s32[]{:S(2)}) async-start(), calls=%async_computation.8 | async-start | bytes 3932160 | tf_op jit(solution)/shard_map/all_gather | solution.py:39
  8.8 115.3 %all-gather.13.cloned.1.call-start = ((), (), s32[]{:S(2)}) async-start(), calls=%async_computation.10 | async-start | bytes 3932160 | tf_op jit(solution)/shard_map/all_gather | solution.py:67
  20.1 60.6 %copy-start.17 = (bf16[768,192]{1,0:T(8,128)(2,1)}, bf16[768,192]{1,0:T(8,128)(2,1)S(1)}, u32[]{:S(2)}) copy-start(bf16[768,192]{1,0:T(8,128)(2,1)S(1)} %all_gather.48) | copy-start | bytes 884740
  76.6 14.1 %copy-start.10 = (bf16[4,512,768]{2,1,0:T(8,128)(2,1)S(1)}, bf16[4,512,768]{2,1,0:T(8,128)(2,1)}, u32[]{:S(2)}) copy-start(bf16[4,512,768]{2,1,0:T(8,128)(2,1)} %all-gather.9.cloned.1.call-done) | copy-start | bytes 9437188
  80.7 59.6 %all-gather.11.cloned.1.call-start = ((), (), s32[]{:S(2)}) async-start(), calls=%async_computation.9 | async-start | bytes 3932160 | tf_op jit(solution)/shard_map/all_gather | solution.py:66
  90.6 30.5 %copy-start.41 = (f32[192]{0:T(256)S(1)}, f32[192]{0:T(256)}, u32[]{:S(2)}) copy-start(f32[192]{0:T(256)} %param.25) | copy-start | bytes 2308
  92.7 257.0 %reduce-scatter.7.cloned.1.call-start = ((), (), s32[]{:S(2)}) async-start(), calls=%async_computation.11 | async-start | bytes 3932160 | tf_op jit(solution)/shard_map/reduce_scatter | solution.py:43
  110.7 11.7 %copy-start.15 = (bf16[768,192]{1,0:T(8,128)(2,1)}, bf16[768,192]{1,0:T(8,128)(2,1)S(1)}, u32[]{:S(2)}) copy-start(bf16[768,192]{1,0:T(8,128)(2,1)S(1)} %all_gather.45) | copy-start | bytes 884740
  147.4 139.0 %copy-start.7 = (bf16[192,768]{0,1:T(8,128)(2,1)S(1)}, bf16[192,768]{0,1:T(8,128)(2,1)}, u32[]{:S(2)}) copy-start(bf16[192,768]{0,1:T(8,128)(2,1)} %all_gather.50) | copy-start | bytes 884740
  286.5 63.3 %copy-start.1 = (bf16[4,128,768]{2,1,0:T(8,128)(2,1)S(1)}, bf16[4,128,768]{2,1,0:T(8,128)(2,1)}, u32[]{:S(2)}) copy-start(bf16[4,128,768]{2,1,0:T(8,128)(2,1)} %param.22) | copy-start | bytes 2359300
  286.5 63.3 %copy-start.20 = (f32[768]{0:T(1024)S(1)}, f32[768]{0:T(1024)}, u32[]{:S(2)}) copy-start(f32[768]{0:T(1024)} %param.30) | copy-start | bytes 9220
  289.2 62.2 %copy-start.21 = (f32[768]{0:T(1024)S(1)}, f32[768]{0:T(1024)}, u32[]{:S(2)}) copy-start(f32[768]{0:T(1024)} %param.31) | copy-start | bytes 9220
  289.2 62.2 %copy-start.36 = (f32[768]{0:T(1024)S(1)}, f32[768]{0:T(1024)}, u32[]{:S(2)}) copy-start(f32[768]{0:T(1024)} %param.32) | copy-start | bytes 9220
  289.2 128.0 %copy-start.37 = (f32[768]{0:T(1024)S(1)}, f32[768]{0:T(1024)}, u32[]{:S(2)}) copy-start(f32[768]{0:T(1024)} %param.34) | copy-start | bytes 9220
  289.3 65.3 %all-gather.17.cloned.1.call-start = ((), (), s32[]{:S(2)}) async-start(), calls=%async_computation.13 | async-start | bytes 1327104 | tf_op jit(solution)/shard_map/all_gather | solution.py:55
  289.8 127.4 %all-gather.15.cloned.1.call-start = ((), (), s32[]{:S(2)}) async-start(), calls=%async_computation.12 | async-start | bytes 3932160 | tf_op jit(solution)/shard_map/all_gather | solution.py:39
  353.9 87.9 %all-gather.19.cloned.1.call-start = ((), (), s32[]{:S(2)}) async-start(), calls=%async_computation.14 | async-start | bytes 1327104 | tf_op jit(solution)/shard_map/all_gather | solution.py:59
  354.5 154.1 %reduce-scatter.9.cloned.1.call-start = ((), (), s32[]{:S(2)}) async-start(), calls=%async_computation.15 | async-start | bytes 3932160 | tf_op jit(solution)/shard_map/reduce_scatter | solution.py:43
  448.4 60.2 %copy-start.2 = (bf16[4,128,768]{2,1,0:T(8,128)(2,1)S(1)}, bf16[4,128,768]{2,1,0:T(8,128)(2,1)}, u32[]{:S(2)}) copy-start(bf16[4,128,768]{2,1,0:T(8,128)(2,1)} %reduce-scatter.7.cloned.1.call-done) | copy-start | bytes 2359300
  448.5 131.1 %all-gather.21.cloned.1.call-start = ((), (), s32[]{:S(2)}) async-start(), calls=%async_computation.16 | async-start | bytes 3932160 | tf_op jit(solution)/shard_map/all_gather | solution.py:39
  510.6 5.7 copy-start.23
  513.1 3.2 copy-start.28
  513.1 3.2 copy-start.29
  516.3 139.2 %reduce-scatter.11.cloned.1.call-start = ((), (), s32[]{:S(2)}) async-start(), calls=%async_computation.17 | async-start | bytes 3932160 | tf_op jit(solution)/shard_map/reduce_scatter | solution.py:43
  579.6 12.7 %copy-start.40 = (bf16[768,768]{1,0:T(8,128)(2,1)S(1)}, bf16[768,768]{1,0:T(8,128)(2,1)}, u32[]{:S(2)}) copy-start(bf16[768,768]{1,0:T(8,128)(2,1)} %all-gather.17.cloned.1.call-done) | copy-start | bytes 3538948
  596.4 130.1 %all-gather.23.cloned.1.call-start = ((), (), s32[]{:S(2)}) async-start(), calls=%async_computation.18 | async-start | bytes 3932160 | tf_op jit(solution)/shard_map/all_gather | solution.py:39
  659.7 66.8 %copy-start.8 = (bf16[192,768]{0,1:T(8,128)(2,1)S(1)}, bf16[192,768]{0,1:T(8,128)(2,1)}, u32[]{:S(2)}) copy-start(bf16[192,768]{0,1:T(8,128)(2,1)} %all_gather.50) | copy-start | bytes 884740
  659.7 70.0 %copy-start.24 = (f32[4,128]{1,0:T(4,128)}, f32[4,128]{1,0:T(4,128)S(1)}, u32[]{:S(2)}) copy-start(f32[4,128]{1,0:T(4,128)S(1)} %broadcast_multiply_fusion) | copy-start | bytes 6148
  659.7 70.0 %copy-start.26 = (f32[4,128]{1,0:T(4,128)}, f32[4,128]{1,0:T(4,128)S(1)}, u32[]{:S(2)}) copy-start(f32[4,128]{1,0:T(4,128)S(1)} %broadcast_multiply_fusion.1) | copy-start | bytes 6148
  663.0 260.4 %reduce-scatter.13.cloned.1.call-start = ((), (), s32[]{:S(2)}) async-start(), calls=%async_computation.19 | async-start | bytes 3932160 | tf_op jit(solution)/shard_map/reduce_scatter | solution.py:283
  726.5 4.1 copy-start.6
  886.9 76.8 %reduce-scatter.15.cloned.1.call-start = ((), (), s32[]{:S(2)}) async-start(), calls=%async_computation.20 | async-start | bytes 3932160 | tf_op jit(solution)/shard_map/reduce_scatter | solution.py:289
  887.7 209.0 %reduce-scatter.17.cloned.1.call-start = ((), (), s32[]{:S(2)}) async-start(), calls=%async_computation.21 | async-start | bytes 3932160 | tf_op jit(solution)/shard_map/reduce_scatter | solution.py:43
  891.6 72.1 %copy-start.18 = (bf16[768,192]{1,0:T(8,128)(2,1)S(1)}, bf16[768,192]{1,0:T(8,128)(2,1)}, u32[]{:S(2)}) copy-start(bf16[768,192]{1,0:T(8,128)(2,1)} %copy-done.17) | copy-start | bytes 884740
  971.3 5.7 copy-start.39
  971.3 5.7 copy-start.43
  984.4 24.4 %all-to-all-start.1 = ((bf16[8,960,96]{1,2,0:T(8,128)(2,1)}), bf16[8,960,96]{1,2,0:T(8,128)(2,1)}, u32[]{:S(2)}, u32[]{:S(2)}) async-start(bf16[8,960,96]{1,2,0:T(8,128)(2,1)} %bitcast.258), calls=%async_computation.7 | async-start | bytes 3145728 | tf_op jit(solution)/shard_map/all_to_all | solution.py:21
  999.4 13.8 %copy-start.30 = (f32[768]{0:T(1024)S(1)}, f32[768]{0:T(1024)}, u32[]{:S(2)}) copy-start(f32[768]{0:T(1024)} %get-tuple-element.224) | copy-start | bytes 9220
  999.4 13.8 %copy-start.31 = (f32[768]{0:T(1024)S(1)}, f32[768]{0:T(1024)}, u32[]{:S(2)}) copy-start(f32[768]{0:T(1024)} %get-tuple-element.233) | copy-start | bytes 9220
  999.4 13.8 %copy-start.32 = (f32[768]{0:T(1024)S(1)}, f32[768]{0:T(1024)}, u32[]{:S(2)}) copy-start(f32[768]{0:T(1024)} %get-tuple-element.283) | copy-start | bytes 9220
  999.4 13.8 %copy-start.33 = (f32[768]{0:T(1024)S(1)}, f32[768]{0:T(1024)}, u32[]{:S(2)}) copy-start(f32[768]{0:T(1024)} %get-tuple-element.222) | copy-start | bytes 9220
  999.4 13.8 %copy-start.34 = (f32[768]{0:T(1024)S(1)}, f32[768]{0:T(1024)}, u32[]{:S(2)}) copy-start(f32[768]{0:T(1024)} %get-tuple-element.229) | copy-start | bytes 9220
  999.4 13.8 %copy-start.35 = (f32[768]{0:T(1024)S(1)}, f32[768]{0:T(1024)}, u32[]{:S(2)}) copy-start(f32[768]{0:T(1024)} %get-tuple-element.285) | copy-start | bytes 9220
  1008.8 84.3 %all-to-all-start = ((bf16[8,96,1344]{2,1,0:T(8,128)(2,1)}), bf16[8,96,1344]{2,1,0:T(8,128)(2,1)}, u32[]{:S(2)}, u32[]{:S(2)}) async-start(bf16[8,96,1344]{2,1,0:T(8,128)(2,1)} %bitcast.255), calls=%async_computation.6 | async-start | bytes 4325376 | tf_op jit(solution)/shard_map/all_to_all | solution.py:21
  1013.2 66.0 %copy-start.38 = (f32[768]{0:T(1024)S(1)}, f32[768]{0:T(1024)}, u32[]{:S(2)}) copy-start(f32[768]{0:T(1024)} %get-tuple-element.316) | copy-start | bytes 9220
  1076.2 20.5 %copy-start.4 = (f32[4,128,768]{2,1,0:T(8,128)S(1)}, f32[4,128,768]{2,1,0:T(8,128)}, u32[]{:S(2)}) copy-start(f32[4,128,768]{2,1,0:T(8,128)} %copy-done.3) | copy-start | bytes 4718596
  1076.2 20.5 %copy-start.25 = (f32[4,128]{1,0:T(4,128)S(1)}, f32[4,128]{1,0:T(4,128)}, u32[]{:S(2)}) copy-start(f32[4,128]{1,0:T(4,128)} %copy-done.24) | copy-start | bytes 6148
  1076.2 20.5 %copy-start.27 = (f32[4,128]{1,0:T(4,128)S(1)}, f32[4,128]{1,0:T(4,128)}, u32[]{:S(2)}) copy-start(f32[4,128]{1,0:T(4,128)} %copy-done.26) | copy-start | bytes 6148
  (23 other events, 47.4 us)
Sparse Core Ops, SparseCore 0:
  10.4 66.1 all-gather.8
  80.9 27.7 all-gather.12
  110.8 29.4 all-gather.10
  289.4 60.3 reduce-scatter.6
  663.2 63.2 all-gather.22
  887.0 36.3 reduce-scatter.12
  926.0 37.7 reduce-scatter.14
Sparse Core Ops, SparseCore 1:
  291.6 23.8 all-gather.16
  354.0 63.2 all-gather.14
  419.0 22.4 all-gather.18
  448.5 60.0 reduce-scatter.8
  516.4 63.1 all-gather.20
  596.4 59.0 reduce-scatter.10
  971.4 60.3 reduce-scatter.16
where the time goes:
time: 1120 us; the launch traced here: 1110 us
  waiting for transfers between devices  512 us (46%)
  matrix products  263 us (23%)
  local copies, waits for them, and re-layouts  128 us (11%)
  blocking collectives  117 us (10%)
  other arithmetic  59.3 us (5%)
  between operations  16.7 us (1%)
    all_gather x4, waiting for transfers between devices, whole_rows(): return lax.all_gather(tensor, 'tp', axis=1, tiled=True)  246 us
    reduce_scatter x4, waiting for transfers between devices, feature_sum(): lax.psum_scatter(tensor.astype(jnp.bfloat16), 'tp', scatter_dimension=1,...  179 us
    psum x1, blocking collectives, per_device(): lax.psum((output_bias_grad, first_gain_grad, first_shift_grad, contract_b...  60.9 us
    dot_general x24, matrix products, masked_scores(): lax.dot_general(query_rows, key_rows, (((1,), (1,)), ((), ())), preferred...  49.7 us
    dot_general x12, matrix products, attend(): jnp.dot(softmax_rows, value_rows, preferred_element_type=jnp.float32)  47.1 us
    dynamic_slice x48, local copies, waits for them, and re-layouts, per_device(): lax.map(attend, (query_items, to_items(keys_all), to_items(values_all), q...  37.8 us
    reduce_scatter x1, waiting for transfers between devices, per_device(): lax.psum_scatter(from_items(values_part, seq_count).astype(jnp.bfloat16),...  35.4 us
    reduce_scatter x1, waiting for transfers between devices, per_device(): lax.psum_scatter(from_items(keys_part, seq_count).astype(jnp.bfloat16), '...  31.8 us
  transfers between devices with their start and end apart: 16, of which 11 were waited for; matrix products, arithmetic and copies ran while one was open for 8% of the time, Pallas kernels for 0%

commit v1 on v0

v1 whole, which is shorter than its diff:
```python
import functools

import jax
import jax.numpy as jnp
from jax import lax
from jax.experimental import pallas as pl
from jax.experimental.pallas import tpu as pltpu
from jax.sharding import PartitionSpec as P

HEAD_DIM = 64
TILE_Q = 256
TILE_K = 256

epsilon = 1e-05
masked_value = -1e30
bf16 = jnp.bfloat16
f32 = jnp.float32


def dot32(a, b, dims):
    return lax.dot_general(a, b, (dims, ((), ())), preferred_element_type=f32)


def swap(value, axis, bit):
    count = lax.axis_size(axis)
    return lax.ppermute(value, axis, [(i, i ^ bit) for i in range(count)])


def side(axis, bit):
    return (lax.axis_index(axis) & bit) != 0


def exchange_blocks(blocks, axis):
    count = lax.axis_size(axis)
    me = lax.axis_index(axis)
    got = []
    for k in range(1, count):
        send = lax.dynamic_index_in_dim(blocks, (me + k) % count, 0, keepdims=True)
        got.append(lax.ppermute(send, axis, [(i, (i + k) % count) for i in range(count)]))
    out = blocks
    for k in range(1, count):
        out = lax.dynamic_update_slice_in_dim(out, got[k - 1], (me - k) % count, 0)
    return out


def gather_line(value, axis):
    count = lax.axis_size(axis)
    me = lax.axis_index(axis)
    got = [
        lax.ppermute(value, axis, [(i, (i + k) % count) for i in range(count)])
        for k in range(1, count)
    ]
    out = jnp.broadcast_to(value[None], (count, *value.shape))
    for k in range(1, count):
        out = lax.dynamic_update_slice_in_dim(out, got[k - 1][None], (me - k) % count, 0)
    return out


def bits_of(axis):
    count = lax.axis_size(axis)
    bits, bit = [], 1
    while bit < count:
        bits.append(bit)
        bit *= 2
    return bits


def exchange_orders():
    ctx_bits = [("ctx", b) for b in bits_of("ctx")]
    fsdp_bits = [("fsdp", b) for b in bits_of("fsdp")]
    near, far = ctx_bits[:1], ctx_bits[1:]
    return (far + fsdp_bits + near, fsdp_bits + far + near)


def gather_rows(local):
    lines = gather_line(local, "tp")
    half = lines.shape[0] // 2
    done = []
    for color, order in enumerate(exchange_orders()):
        part = lines[color * half : (color + 1) * half]
        names = []
        for axis, bit in order:
            other = swap(part, axis, bit)
            mine_last = side(axis, bit)
            names.append((axis, bit))
            names.sort(key=lambda n: (n[0] == "ctx", -n[1]))
            at = 1 + names.index((axis, bit))
            part = jnp.where(
                mine_last, jnp.stack([other, part], at), jnp.stack([part, other], at)
            )
        done.append(part.reshape(half, -1, local.shape[1]))
    return jnp.concatenate(done, 0)


def scatter_rows(whole, rows):
    half = whole.shape[0] // 2
    left = []
    for color, order in enumerate(exchange_orders()):
        names = sorted(order, key=lambda n: (n[0] == "ctx", -n[1]))
        part = whole[color * half : (color + 1) * half]
        part = part.reshape(half, *([2] * len(names)), rows, whole.shape[2])
        for axis, bit in reversed(order):
            at = 1 + names.index((axis, bit))
            names.remove((axis, bit))
            low = lax.index_in_dim(part, 0, at, keepdims=False)
            high = lax.index_in_dim(part, 1, at, keepdims=False)
            upper = side(axis, bit)
            keep, send = jnp.where(upper, high, low), jnp.where(upper, low, high)
            other = swap(send, axis, bit)
            part = (keep.astype(f32) + other.astype(f32)).astype(bf16)
        left.append(part)
    lines = exchange_blocks(jnp.concatenate(left, 0), "tp")
    return jnp.sum(lines.astype(f32), axis=0)


def sum_everywhere(value):
    for axis in ("ctx", "fsdp", "tp"):
        for bit in bits_of(axis):
            value = value + swap(value, axis, bit)
    return value


def head_rows(value, head):
    row = lax.broadcasted_iota(jnp.int32, value.shape, 0)
    return jnp.where((row >= head * HEAD_DIM) & (row < (head + 1) * HEAD_DIM), value, 0)


def head_cols(value, head):
    col = lax.broadcasted_iota(jnp.int32, value.shape, 1)
    return jnp.where((col >= head * HEAD_DIM) & (col < (head + 1) * HEAD_DIM), value, 0)


def attend_kernel(
    low_ref, high_ref, q_ref, k_ref, v_ref, segr_ref, segc_ref, att_ref, attt_ref, lse_ref,
    vt_ref, acc_ref,
):
    tokens, width = q_ref.shape
    heads = width // HEAD_DIM
    scale = HEAD_DIM ** (-0.5)

    def turn(i, carry):
        at = pl.multiple_of(i * TILE_K, TILE_K)
        vt_ref[:, pl.ds(at, TILE_K)] = v_ref[pl.ds(at, TILE_K), :].astype(f32).T.astype(bf16)
        return carry

    lax.fori_loop(0, tokens // TILE_K, turn, 0)

    def one_q(i, carry):
        qa = pl.multiple_of(i * TILE_Q, TILE_Q)
        qt = (q_ref[pl.ds(qa, TILE_Q), :].astype(f32) * scale).T
        qts = [head_rows(qt, h).astype(bf16) for h in range(heads)]
        seg_q = segr_ref[:, pl.ds(qa, TILE_Q)]
        acc_ref[...] = jnp.zeros_like(acc_ref)

        def one_k(j, state):
            ka = pl.multiple_of(j * TILE_K, TILE_K)
            keys = k_ref[pl.ds(ka, TILE_K), :]
            same = segc_ref[pl.ds(ka, TILE_K), :] == seg_q
            tops, sums = [], []
            for h in range(heads):
                rows = slice(h * HEAD_DIM, (h + 1) * HEAD_DIM)
                s = jnp.where(same, dot32(keys, qts[h], ((1,), (0,))), masked_value)
                top = jnp.maximum(state[0][h], jnp.max(s, axis=0, keepdims=True))
                shrink = jnp.exp(state[0][h] - top)
                p = jnp.exp(s - top)
                sums.append(state[1][h] * shrink + jnp.sum(p, axis=0, keepdims=True))
                tops.append(top)
                pv = dot32(vt_ref[rows, pl.ds(ka, TILE_K)], p.astype(bf16), ((1,), (0,)))
                acc_ref[rows, :] = acc_ref[rows, :] * shrink + pv
            return (tuple(tops), tuple(sums))

        init = (
            tuple(jnp.full((1, TILE_Q), masked_value, f32) for _ in range(heads)),
            tuple(jnp.zeros((1, TILE_Q), f32) for _ in range(heads)),
        )
        tops, sums = lax.fori_loop(low_ref[i], high_ref[i], one_k, init)
        for h in range(heads):
            rows = slice(h * HEAD_DIM, (h + 1) * HEAD_DIM)
            acc_ref[rows, :] = acc_ref[rows, :] / sums[h]
            lse_ref[h : h + 1, pl.ds(qa, TILE_Q)] = tops[h] + jnp.log(sums[h])
        attt_ref[:, pl.ds(qa, TILE_Q)] = acc_ref[...]
        att_ref[pl.ds(qa, TILE_Q), :] = acc_ref[...].T.astype(bf16)
        return carry

    lax.fori_loop(0, tokens // TILE_Q, one_q, 0)


def attend_back_kernel(
    low_ref, high_ref, q_ref, k_ref, v_ref, do_ref, attt_ref, lse_ref, segr_ref, segc_ref,
    dq_ref, dk_ref, dv_ref, kt_ref, dqt_ref, dka_ref, dva_ref,
):
    tokens, width = q_ref.shape
    heads = width // HEAD_DIM
    scale = HEAD_DIM ** (-0.5)

    def turn(i, carry):
        at = pl.multiple_of(i * TILE_K, TILE_K)
        kt_ref[:, pl.ds(at, TILE_K)] = k_ref[pl.ds(at, TILE_K), :].astype(f32).T.astype(bf16)
        return carry

    lax.fori_loop(0, tokens // TILE_K, turn, 0)
    dka_ref[...] = jnp.zeros_like(dka_ref)
    dva_ref[...] = jnp.zeros_like(dva_ref)

    def one_q(i, carry):
        qa = pl.multiple_of(i * TILE_Q, TILE_Q)
        q = q_ref[pl.ds(qa, TILE_Q), :].astype(f32) * scale
        do = do_ref[pl.ds(qa, TILE_Q), :].astype(f32)
        qt, dot_ = q.T, do.T
        qs = [head_cols(q, h).astype(bf16) for h in range(heads)]
        dos = [head_cols(do, h).astype(bf16) for h in range(heads)]
        qts = [head_rows(qt, h).astype(bf16) for h in range(heads)]
        dots = [head_rows(dot_, h).astype(bf16) for h in range(heads)]
        prod = dot_ * attt_ref[:, pl.ds(qa, TILE_Q)]
        deltas = [
            jnp.sum(prod[h * HEAD_DIM : (h + 1) * HEAD_DIM, :], axis=0, keepdims=True)
            for h in range(heads)
        ]
        lses = [lse_ref[h : h + 1, pl.ds(qa, TILE_Q)] for h in range(heads)]
        seg_q = segr_ref[:, pl.ds(qa, TILE_Q)]
        dqt_ref[...] = jnp.zeros_like(dqt_ref)

        def one_k(j, state):
            ka = pl.multiple_of(j * TILE_K, TILE_K)
            keys = k_ref[pl.ds(ka, TILE_K), :]
            values = v_ref[pl.ds(ka, TILE_K), :]
            same = segc_ref[pl.ds(ka, TILE_K), :] == seg_q
            dk = dka_ref[pl.ds(ka, TILE_K), :]
            dv = dva_ref[pl.ds(ka, TILE_K), :]
            for h in range(heads):
                rows = slice(h * HEAD_DIM, (h + 1) * HEAD_DIM)
                s = jnp.where(same, dot32(keys, qts[h], ((1,), (0,))), masked_value)
                p = jnp.exp(s - lses[h])
                dp = dot32(values, dots[h], ((1,), (0,)))
                ds = (p * (dp - deltas[h])).astype(bf16)
                dv = dv + dot32(p.astype(bf16), dos[h], ((1,), (0,)))
                dk = dk + dot32(ds, qs[h], ((1,), (0,)))
                dqt_ref[rows, :] += dot32(kt_ref[rows, pl.ds(ka, TILE_K)], ds, ((1,), (0,)))
            dka_ref[pl.ds(ka, TILE_K), :] = dk
            dva_ref[pl.ds(ka, TILE_K), :] = dv
            return state

        lax.fori_loop(low_ref[i], high_ref[i], one_k, 0)
        dq_ref[pl.ds(qa, TILE_Q), :] = (dqt_ref[...] * scale).T.astype(bf16)
        return carry

    lax.fori_loop(0, tokens // TILE_Q, one_q, 0)
    dk_ref[...] = dka_ref[...].astype(bf16)
    dv_ref[...] = dva_ref[...].astype(bf16)


smem_spec = pl.BlockSpec(memory_space=pltpu.SMEM)
vmem_spec = pl.BlockSpec(memory_space=pltpu.VMEM)


def attend(lows, highs, q, k, v, seg_row, seg_col):
    tokens, width = q.shape
    return pl.pallas_call(
        attend_kernel,
        in_specs=[smem_spec] * 2 + [vmem_spec] * 5,
        out_specs=[vmem_spec] * 3,
        out_shape=[
            jax.ShapeDtypeStruct((tokens, width), bf16),
            jax.ShapeDtypeStruct((width, tokens), f32),
            jax.ShapeDtypeStruct((8, tokens), f32),
        ],
        scratch_shapes=[pltpu.VMEM((width, tokens), bf16), pltpu.VMEM((width, TILE_Q), f32)],
        name="attend",
    )(lows, highs, q, k, v, seg_row, seg_col)


def attend_back(lows, highs, q, k, v, do, attt, lse, seg_row, seg_col):
    tokens, width = q.shape
    return pl.pallas_call(
        attend_back_kernel,
        in_specs=[smem_spec] * 2 + [vmem_spec] * 8,
        out_specs=[vmem_spec] * 3,
        out_shape=[jax.ShapeDtypeStruct((tokens, width), bf16)] * 3,
        scratch_shapes=[
            pltpu.VMEM((width, tokens), bf16),
            pltpu.VMEM((width, TILE_Q), f32),
            pltpu.VMEM((tokens, width), f32),
            pltpu.VMEM((tokens, width), f32),
        ],
        name="attend_back",
    )(lows, highs, q, k, v, do, attt, lse, seg_row, seg_col)


def exact_gelu(values):
    return jax.nn.gelu(values, approximate=False)


def norm_forward(resid, gain, shift):
    row_mean = jnp.mean(resid, axis=1, keepdims=True)
    spread = jnp.mean(resid * resid, axis=1, keepdims=True) - row_mean * row_mean
    inverse = lax.rsqrt(spread + epsilon)
    normed = (resid - row_mean) * inverse
    return (normed * gain + shift, normed, inverse)


def norm_backward(upstream, normed, inverse, gain):
    scaled = upstream * gain
    first_mean = jnp.mean(scaled, axis=1, keepdims=True)
    second_mean = jnp.mean(scaled * normed, axis=1, keepdims=True)
    back_term = inverse * (scaled - first_mean - normed * second_mean)
    return (back_term, jnp.sum(upstream * normed, axis=0), jnp.sum(upstream, axis=0))


def token_sum(tensor):
    return jnp.sum(tensor.astype(f32), axis=0)


def per_device(
    inputs,
    segments,
    query_weight,
    query_bias,
    key_weight,
    value_weight,
    value_bias,
    output_weight,
    output_bias,
    first_gain,
    first_shift,
    expand_weight,
    expand_bias,
    contract_weight,
    contract_bias,
    second_gain,
    second_shift,
    cotangent,
):
    seq_count, rows_here, features = inputs.shape
    lines = lax.axis_size("tp")
    blocks = lax.axis_size("ctx")
    width = query_weight.shape[1]
    hidden = expand_weight.shape[1]
    shard = query_weight.shape[0]
    assert seq_count == lines and blocks == lines
    tokens = segments.shape[1]
    here = rows_here * lines
    groups = range(lines)

    front = gather_rows(jnp.concatenate([query_weight, key_weight, value_weight], 1))
    biases = gather_line(jnp.concatenate([query_bias, value_bias, expand_bias]), "tp")
    x = exchange_blocks(inputs, "tp").reshape(here, features)
    back = gather_rows(
        jnp.concatenate([expand_weight, contract_weight.T, output_weight.T], 1)
    )
    expand = [back[t, :, :hidden] for t in groups]
    contract = [back[t, :, hidden : 2 * hidden] for t in groups]
    output = [back[t, :, 2 * hidden :] for t in groups]

    seg = lax.dynamic_index_in_dim(segments, lax.axis_index("tp"), 0, keepdims=False)
    firsts, lasts = seg[::TILE_Q], seg[TILE_Q - 1 :: TILE_Q]
    before = jnp.sum((seg[None, :] < firsts[:, None]).astype(jnp.int32), axis=1)
    until = jnp.sum((seg[None, :] <= lasts[:, None]).astype(jnp.int32), axis=1)
    lows, highs = before // TILE_K, (until + TILE_K - 1) // TILE_K
    seg_row, seg_col = seg[None, :], seg[:, None]

    none = jnp.zeros((width,), f32)
    projected = jnp.stack(
        [
            (
                dot32(x, front[t], ((1,), (0,)))
                + jnp.concatenate([biases[t, :width], none, biases[t, width : 2 * width]])
            ).astype(bf16)
            for t in groups
        ]
    )
    qkv = exchange_blocks(projected, "ctx").reshape(tokens, 3 * width)
    q, k, v = qkv[:, :width], qkv[:, width : 2 * width], qkv[:, 2 * width :]
    att, attt, lse = attend(lows, highs, q, k, v, seg_row, seg_col)
    att = exchange_blocks(att.reshape(blocks, here, width), "ctx")
    branch = output_bias + sum(dot32(att[t], output[t], ((1,), (1,))) for t in groups)
    middle, middle_normed, middle_inverse = norm_forward(
        x.astype(f32) + branch, first_gain, first_shift
    )
    middle_low = middle.astype(bf16)
    actives, pulls = [], []
    for t in groups:
        preact = dot32(middle_low, expand[t], ((1,), (0,))) + biases[t, 2 * width :]
        active, pull = jax.vjp(exact_gelu, preact)
        actives.append(active.astype(bf16))
        pulls.append(pull)
    feedforward = contract_bias + sum(
        dot32(actives[t], contract[t], ((1,), (1,))) for t in groups
    )
    outputs, final_normed, final_inverse = norm_forward(
        middle + feedforward, second_gain, second_shift
    )
    outputs = exchange_blocks(
        outputs.astype(bf16).reshape(lines, rows_here, features), "tp"
    )

    upstream = exchange_blocks(cotangent, "tp").reshape(here, features).astype(f32)
    final_grad, second_gain_grad, second_shift_grad = norm_backward(
        upstream, final_normed, final_inverse, second_gain
    )
    feed_grad = final_grad.astype(bf16)
    contract_bias_grad = token_sum(feed_grad)
    expand_bias_grads, expand_parts, contract_parts, output_parts = [], [], [], []
    middle_grad = final_grad
    for t in groups:
        active_grad = dot32(feed_grad, contract[t], ((1,), (0,)))
        preact_grad = pulls[t](active_grad)[0].astype(bf16)
        expand_bias_grads.append(token_sum(preact_grad))
        contract_parts.append(dot32(feed_grad, actives[t], ((0,), (0,))).astype(bf16))
        expand_parts.append(dot32(middle_low, preact_grad, ((0,), (0,))).astype(bf16))
        middle_grad = middle_grad + dot32(preact_grad, expand[t], ((1,), (1,)))
    resid_grad, first_gain_grad, first_shift_grad = norm_backward(
        middle_grad, middle_normed, middle_inverse, first_gain
    )
    branch_grad = resid_grad.astype(bf16)
    output_bias_grad = token_sum(branch_grad)
    for t in groups:
        output_parts.append(dot32(branch_grad, att[t], ((0,), (0,))).astype(bf16))
    att_grad = jnp.stack(
        [dot32(branch_grad, output[t], ((1,), (0,))).astype(bf16) for t in groups]
    )
    do = exchange_blocks(att_grad, "ctx").reshape(tokens, width)
    dq, dk, dv = attend_back(lows, highs, q, k, v, do, attt, lse, seg_row, seg_col)
    projected_grad = exchange_blocks(
        jnp.concatenate([dq, dk, dv], 1).reshape(blocks, here, 3 * width), "ctx"
    )
    back_grad = scatter_rows(
        jnp.stack(
            [
                jnp.concatenate([expand_parts[t], contract_parts[t], output_parts[t]], 1)
                for t in groups
            ]
        ),
        shard,
    )
    front_grad = scatter_rows(
        jnp.stack([dot32(x, projected_grad[t], ((0,), (0,))).astype(bf16) for t in groups]),
        shard,
    )
    input_grad = resid_grad + sum(
        dot32(projected_grad[t], front[t], ((1,), (1,))) for t in groups
    )
    input_grad = exchange_blocks(
        input_grad.astype(bf16).reshape(lines, rows_here, features), "tp"
    )

    early = sum_everywhere(
        jnp.concatenate(
            [
                output_bias_grad,
                first_gain_grad,
                first_shift_grad,
                contract_bias_grad,
                second_gain_grad,
                second_shift_grad,
                *expand_bias_grads,
            ]
        )
    )
    late = sum_everywhere(jnp.sum(projected_grad.astype(f32), axis=1))
    line = lax.axis_index("tp")
    own = lax.dynamic_index_in_dim(late, line, 0, keepdims=False)
    whole = early[: 6 * features].reshape(6, features)
    expand_bias_grad = lax.dynamic_slice_in_dim(early, 6 * features + line * hidden, hidden, 0)
    return (
        outputs,
        input_grad,
        front_grad[:, :width],
        own[:width],
        front_grad[:, width : 2 * width],
        front_grad[:, 2 * width :],
        own[2 * width :],
        back_grad[:, 2 * hidden :].T,
        whole[0],
        whole[1],
        whole[2],
        back_grad[:, :hidden],
        expand_bias_grad,
        back_grad[:, hidden : 2 * hidden].T,
        whole[3],
        whole[4],
        whole[5],
    )


def solution(mesh):
    rows = P("fsdp", ("ctx", "tp"), None)
    front, back = P(("fsdp", "ctx"), "tp"), P("tp", ("fsdp", "ctx"))
    return jax.shard_map(
        per_device,
        mesh=mesh,
        in_specs=(
            rows, P("fsdp", None), front, P("tp"), front, front, P("tp"), back, P(), P(), P(),
            front, P("tp"), back, P(), P(), P(), rows,
        ),
        out_specs=(
            rows, rows, front, P("tp"), front, front, P("tp"), back, P(), P(), P(),
            front, P("tp"), back, P(), P(), P(),
        ),
        check_vma=False,
    )
```

time: 1120 us -> 623 us (0.56)
  waiting for transfers between devices: 512 us -> 198 us
  matrix products: 263 us -> 108 us
  blocking collectives: 117 us -> 0 us
  starting transfers between devices: 10.1 us -> 107 us
  Pallas kernels: 0 us -> 73.3 us
  local copies, waits for them, and re-layouts: 128 us -> 74.6 us
  between operations: 16.7 us -> 2.67 us
    all_gather x8 -> x0, waiting for transfers between devices: 255 us -> none  [the longest x4 246 us: whole_rows(): return lax.all_gather(tensor, 'tp', axis=1, tiled=True)]
    reduce_scatter x6 -> x0, waiting for transfers between devices: 246 us -> none  [the longest x4 179 us: feature_sum(): lax.psum_scatter(tensor.astype(jnp.bfloat16), 'tp', scatter_dimension=1,...]
    ppermute x0 -> x73, waiting for transfers between devices: none -> 198 us  [the longest x30 86.7 us: exchange_blocks(): lax.ppermute(send, axis, [(i, (i + k) % count) for i in range(count)])]
    dot_general x102 -> x48, matrix products: 263 us -> 108 us  [dot32(): return lax.dot_general(a, b, (dims, ((), ())), preferred_element_type=f32)]
    ppermute x0 -> x73, starting transfers between devices: none -> 107 us  [the longest x34 46.6 us: swap(): return lax.ppermute(value, axis, [(i, i ^ bit) for i in range(count)])]
    psum x2 -> x0, blocking collectives: 74.8 us -> none  [the longest x1 60.9 us: per_device(): lax.psum((output_bias_grad, first_gain_grad, first_shift_grad, contract_b...]
    pallas_call x0 -> x2, Pallas kernels: none -> 73.3 us  [the longest x1 37.7 us: attend(): pl.pallas_call(attend_kernel, in_specs=[smem_spec] * 2 + [vmem_spec] * 5,...]
    all_gather x4 -> x0, blocking collectives: 42.2 us -> none  [the longest x1 11.3 us: fetch_weights(): lax.all_gather(value_weight, ('fsdp', 'ctx'), axis=0, tiled=True)]
  transfers between devices with their start and end apart: 16 -> 73, of which waited for: 11 -> 36; matrix products, arithmetic and copies ran while one was open for 8% -> 22% of each run, Pallas kernels for 0% -> 12%
where the time goes in v1:
time: 623 us; the launch traced here: 615 us
  waiting for transfers between devices  198 us (32%)
  matrix products  108 us (17%)
  starting transfers between devices  107 us (17%)
  local copies, waits for them, and re-layouts  74.6 us (12%)
  Pallas kernels  73.3 us (12%)
  other arithmetic  52.4 us (8%)
    dot_general x48, matrix products, dot32(): return lax.dot_general(a, b, (dims, ((), ())), preferred_element_type=f32)  108 us
    ppermute x30, waiting for transfers between devices, exchange_blocks(): lax.ppermute(send, axis, [(i, (i + k) % count) for i in range(count)])  86.7 us
    ppermute x34, waiting for transfers between devices, swap(): return lax.ppermute(value, axis, [(i, i ^ bit) for i in range(count)])  79.8 us
    ppermute x34, starting transfers between devices, swap(): return lax.ppermute(value, axis, [(i, i ^ bit) for i in range(count)])  46.6 us
    ppermute x30, starting transfers between devices, exchange_blocks(): lax.ppermute(send, axis, [(i, (i + k) % count) for i in range(count)])  39.5 us
    pallas_call x1, Pallas kernels, attend(): pl.pallas_call(attend_kernel, in_specs=[smem_spec] * 2 + [vmem_spec] * 5,...  37.7 us
    pallas_call x1, Pallas kernels, attend_back(): pl.pallas_call(attend_back_kernel, in_specs=[smem_spec] * 2 + [vmem_spec]...  35.5 us
    ppermute x9, waiting for transfers between devices, gather_line(): lax.ppermute(value, axis, [(i, (i + k) % count) for i in range(count)])  31.3 us
  transfers between devices with their start and end apart: 73, of which 36 were waited for; matrix products, arithmetic and copies ran while one was open for 22% of the time, Pallas kernels for 12%

profile of v1, /device:TPU:0, one launch (start us, length us, event | category | flops | bytes accessed | tf_op | source)
XLA Modules:
  0.0 615.4 jit_solution(1957870837268859957)
XLA Ops:
  2.4 3.1 collective-permute-start.21
  14.6 8.9 %collective-permute-done.9 = f32[1152]{0:T(1024)} collective-permute-done((f32[1152]{0:T(1024)S(1)}, f32[1152]{0:T(1024)}, u32[]{:S(2)}, u32[]{:S(2)}) %collective-permute-start.9) | collective-permute-done | bytes 4640 | tf_op jit(solution)/shard_map/ppermute | solution.py:50
  24.3 6.8 %collective-permute-done.10 = f32[1152]{0:T(1024)} collective-permute-done((f32[1152]{0:T(1024)S(1)}, f32[1152]{0:T(1024)}, u32[]{:S(2)}, u32[]{:S(2)}) %collective-permute-start.10) | collective-permute-done | bytes 4640 | tf_op jit(solution)/shard_map/ppermute | solution.py:50
  31.1 6.9 %collective-permute-start.3 = (bf16[96,576]{1,0:T(8,128)(2,1)S(1)}, bf16[96,576]{1,0:T(8,128)(2,1)}, u32[]{:S(2)}, u32[]{:S(2)}) collective-permute-start(bf16[96,576]{1,0:T(8,128)(2,1)S(1)} %pad_maximum_fusion.18), channel_id=1, source_target_pairs={{0,1},{1,2},{2,3},{3,0},{4,5},{5,6},{6,7},{7,4},{8,9},{9,10},{10,1... | collective-permute-start | bytes 331784 | tf_op jit(solution)/shard_map/ppermute | solution.py:50
  38.7 4.1 collective-permute-start.4
  43.1 9.1 %collective-permute-done.3 = bf16[96,576]{1,0:T(8,128)(2,1)} collective-permute-done((bf16[96,576]{1,0:T(8,128)(2,1)S(1)}, bf16[96,576]{1,0:T(8,128)(2,1)}, u32[]{:S(2)}, u32[]{:S(2)}) %collective-permute-start.3) | collective-permute-done | bytes 110624 | tf_op jit(solution)/shard_map/ppermute | solution.py:50
  53.2 6.3 %collective-permute-done.4 = bf16[96,576]{1,0:T(8,128)(2,1)} collective-permute-done((bf16[96,576]{1,0:T(8,128)(2,1)S(1)}, bf16[96,576]{1,0:T(8,128)(2,1)}, u32[]{:S(2)}, u32[]{:S(2)}) %collective-permute-start.4) | collective-permute-done | bytes 110624 | tf_op jit(solution)/shard_map/ppermute | solution.py:50
  61.4 7.1 %collective-permute-done = bf16[1,128,768]{2,1,0:T(8,128)(2,1)S(1)} collective-permute-done((bf16[1,128,768]{2,1,0:T(8,128)(2,1)S(1)}, bf16[1,128,768]{2,1,0:T(8,128)(2,1)S(1)}, u32[]{:S(2)}, u32[]{:S(2)}) %collective-permute-start) | collective-permute-done | bytes 196640 | tf_op jit(solution)/shard_map/ppermute | solution.py:39
  86.9 4.5 collective-permute-done.34
  94.0 8.7 %collective-permute-done.7 = bf16[2,2,96,576]{3,2,0,1:T(8,128)(2,1)S(1)} collective-permute-done((bf16[2,2,96,576]{3,2,0,1:T(8,128)(2,1)S(1)}, bf16[2,2,96,576]{3,2,0,1:T(8,128)(2,1)S(1)}, u32[]{:S(2)}, u32[]{:S(2)}) %collective-permute-start.7) | collective-permute-done | bytes 442400 | tf_op jit(solution)/shard_map/ppermute | solution.py:26
  113.7 12.2 %collective-permute-done.15 = bf16[1,512,576]{1,2,0:T(8,128)(2,1)S(1)} collective-permute-done((bf16[1,512,576]{1,2,0:T(8,128)(2,1)S(1)}, bf16[1,512,576]{1,2,0:T(8,128)(2,1)S(1)}, u32[]{:S(2)}, u32[]{:S(2)}) %collective-permute-start.15) | collective-permute-done | bytes 589856 | tf_op jit(solution)/shard_map/ppermute | solution.py:39
  127.6 9.2 %collective-permute-done.25 = bf16[2,2,96,1728]{3,2,0,1:T(8,128)(2,1)S(1)} collective-permute-done((bf16[2,2,96,1728]{3,2,0,1:T(8,128)(2,1)S(1)}, bf16[2,2,96,1728]{3,2,0,1:T(8,128)(2,1)S(1)}, u32[]{:S(2)}, u32[]{:S(2)}) %collective-permute-start.25) | collective-permute-done | bytes 1327136 | tf_op jit(solution)/shard_map/ppermute | solution.py:26
  146.7 10.7 %collective-permute-start.29 = (bf16[2,2,2,96,1728]{4,3,1,0,2:T(8,128)(2,1)}, bf16[2,2,2,96,1728]{4,3,1,0,2:T(8,128)(2,1)}, u32[]{:S(2)}, u32[]{:S(2)}) collective-permute-start(bf16[2,2,2,96,1728]{4,3,1,0,2:T(8,128)(2,1)} %maximum_select_fusion.4), channel_id=1, source_target_pairs={{0,4},{4,0},{8,12},{12,8},{1,5},{5,1},{9,13},{13,9},{2,6},{6,2},{1... | collective-permute-start | bytes 7962632 | tf_op jit(solution)/shard_map/ppermute | solution.py:26
  157.5 10.5 %collective-permute-done.17 = bf16[1,512,576]{1,2,0:T(8,128)(2,1)S(1)} collective-permute-done((bf16[1,512,576]{1,2,0:T(8,128)(2,1)S(1)}, bf16[1,512,576]{1,2,0:T(8,128)(2,1)S(1)}, u32[]{:S(2)}, u32[]{:S(2)}) %collective-permute-start.17) | collective-permute-done | bytes 589856 | tf_op jit(solution)/shard_map/ppermute | solution.py:39
  170.7 4.3 fusion.103
  175.0 37.7 %attend.1 = (bf16[2048,192]{1,0:T(8,128)(2,1)}, f32[192,2048]{1,0:T(8,128)}, f32[8,2048]{1,0:T(8,128)}) custom-call(s32[8]{0:T(128)} %get-tuple-element.233.low_ref, s32[8]{0:T(128)} %get-tuple-element.232.high_ref, bf16[2048,192]{1,0:T(8,128)(2,1)} %get-tuple-element.136.q_ref, bf16[2048,192]{1,0:T(8,128)(2,1)} %get-tuple-element.135.k_ref, ...), custom_call_target="tpu_custom_call" | custom-call | tf_op jit(solution)/shard_map/attend/pallas_call | solution.py:258
  216.6 3.0 collective-permute-done.18
  220.8 5.4 collective-permute-done.19
  228.0 4.0 maximum_select_fusion
  238.3 11.0 %multiply_convert_fusion.2 = (bf16[512,768]{1,0:T(8,128)(2,1)S(1)}, f32[512,768]{1,0:T(8,128)S(1)}, f32[512,768]{1,0:T(8,128)}) fusion(f32[768]{0:T(1024)S(1)} %get-tuple-element.111, bf16[512,768]{1,0:T(8,128)(2,1)S(1)} %fusion.39, bf16[2,768,1728]{2,1,0:T(8,128)(2,1)S(1)} %bitcast.419), kind=kOutput, calls=%fused_computation.115 | convolution fusion | flops 629932032 | bytes 5902336 | tf_op jit(solution)/shard_map/dot_general | solution.py:21
  250.1 10.2 %multiply_convert_fusion.3 = (bf16[512,768]{1,0:T(8,128)(2,1)S(1)}, f32[512,768]{1,0:T(8,128)S(1)}, f32[512,768]{1,0:T(8,128)S(1)}) fusion(f32[768]{0:T(1024)S(1)} %get-tuple-element.112, bf16[512,768]{1,0:T(8,128)(2,1)S(1)} %fusion.39, bf16[2,768,1728]{2,1,0:T(8,128)(2,1)S(1)} %bitcast.421), kind=kOutput, calls=%fused_computation.128 | convolution fusion | flops 629932032 | bytes 5902336 | tf_op jit(solution)/shard_map/dot_general | solution.py:21
  261.1 22.6 %multiply_convert_fusion.1 = (bf16[512,768]{1,0:T(8,128)(2,1)S(1)}, f32[512,768]{1,0:T(8,128)S(1)}, f32[512,768]{1,0:T(8,128)S(1)}) fusion(f32[768]{0:T(1024)S(1)} %get-tuple-element.110, bf16[512,768]{1,0:T(8,128)(2,1)S(1)} %fusion.39, bf16[2,768,1728]{2,1,0:T(8,128)(2,1)S(1)} %bitcast.402), kind=kOutput, calls=%fused_computation.102 | convolution fusion | flops 629932032 | bytes 5902336 | tf_op jit(solution)/shard_map/dot_general | solution.py:21
  284.6 10.2 %multiply_convert_fusion = (bf16[512,768]{1,0:T(8,128)(2,1)S(1)}, f32[512,768]{1,0:T(8,128)S(1)}, f32[512,768]{1,0:T(8,128)S(1)}) fusion(f32[768]{0:T(1024)S(1)} %get-tuple-element.109, bf16[512,768]{1,0:T(8,128)(2,1)S(1)} %fusion.39, bf16[2,768,1728]{2,1,0:T(8,128)(2,1)S(1)} %bitcast.404), kind=kOutput, calls=%fused_computation.89 | convolution fusion | flops 629932032 | bytes 5902336 | tf_op jit(solution)/shard_map/dot_general | solution.py:21
  328.8 4.2 copy.194
  334.9 4.3 copy.202
  341.1 4.3 copy.201
  348.4 2.9 collective-permute-start.30
  361.5 3.1 collective-permute-start.70
  369.1 4.5 copy.193
  373.5 4.2 collective-permute-start.72
  380.9 35.5 %attend_back.1 = (bf16[2048,192]{1,0:T(8,128)(2,1)}, bf16[2048,192]{1,0:T(8,128)(2,1)}, bf16[2048,192]{1,0:T(8,128)(2,1)}) custom-call(s32[8]{0:T(128)} %get-tuple-element.233.low_ref, s32[8]{0:T(128)} %get-tuple-element.232.high_ref, bf16[2048,192]{1,0:T(8,128)(2,1)} %get-tuple-element.136.q_ref, bf16[2048,192]{1,0:T(8,128)(2,1)} %get-tuple-element.135.k_ref, ...), custom_call_target="tpu_custom_call" | custom-call | tf_op jit(solution)/shard_map/attend_back/pallas_call | solution.py:274
  416.5 2.9 pad_maximum_fusion.6
  426.0 3.9 select_bitcast_fusion.1
  437.0 7.6 %collective-permute-done.31 = bf16[1,128,768]{2,1,0:T(8,128)(2,1)} collective-permute-done((bf16[1,128,768]{2,1,0:T(8,128)(2,1)}, bf16[1,128,768]{2,1,0:T(8,128)(2,1)}, u32[]{:S(2)}, u32[]{:S(2)}) %collective-permute-start.31) | collective-permute-done | bytes 196640 | tf_op jit(solution)/shard_map/ppermute | solution.py:39
  472.7 3.3 add_convert_fusion
  486.1 3.0 collective-permute-start.42
  489.5 4.5 collective-permute-done.57
  502.8 7.5 %collective-permute-done.43 = bf16[1,128,768]{2,1,0:T(8,128)(2,1)S(1)} collective-permute-done((bf16[1,128,768]{2,1,0:T(8,128)(2,1)S(1)}, bf16[1,128,768]{2,1,0:T(8,128)(2,1)S(1)}, u32[]{:S(2)}, u32[]{:S(2)}) %collective-permute-start.43) | collective-permute-done | bytes 196640 | tf_op jit(solution)/shard_map/ppermute | solution.py:39
  514.6 11.4 %collective-permute-done.46 = bf16[2,2,96,576]{3,2,1,0:T(8,128)(2,1)S(1)} collective-permute-done((bf16[2,2,96,576]{3,2,1,0:T(8,128)(2,1)S(1)}, bf16[2,2,96,576]{3,2,1,0:T(8,128)(2,1)S(1)}, u32[]{:S(2)}, u32[]{:S(2)}) %collective-permute-start.46) | collective-permute-done | bytes 442400 | tf_op jit(solution)/shard_map/ppermute | solution.py:26
  528.6 5.2 collective-permute-done.47
  543.0 4.5 collective-permute-start.52
  547.5 5.2 collective-permute-done.52
  552.7 16.0 %collective-permute-done.60 = bf16[2,2,96,1728]{3,2,1,0:T(8,128)(2,1)S(1)} collective-permute-done((bf16[2,2,96,1728]{3,2,1,0:T(8,128)(2,1)S(1)}, bf16[2,2,96,1728]{3,2,1,0:T(8,128)(2,1)S(1)}, u32[]{:S(2)}, u32[]{:S(2)}) %collective-permute-start.60) | collective-permute-done | bytes 1327136 | tf_op jit(solution)/shard_map/ppermute | solution.py:26
  570.4 4.0 collective-permute-done.63
  576.8 9.6 %collective-permute-done.61 = bf16[2,96,1728]{2,1,0:T(8,128)(2,1)S(1)} collective-permute-done((bf16[2,96,1728]{2,1,0:T(8,128)(2,1)S(1)}, bf16[2,96,1728]{2,1,0:T(8,128)(2,1)S(1)}, u32[]{:S(2)}, u32[]{:S(2)}) %collective-permute-start.61) | collective-permute-done | bytes 663584 | tf_op jit(solution)/shard_map/ppermute | solution.py:26
  588.1 5.9 collective-permute-start.66
  596.5 5.1 collective-permute-done.65
  601.7 11.5 %collective-permute-done.66 = bf16[1,96,1728]{2,1,0:T(8,128)(2,1)S(1)} collective-permute-done((bf16[1,96,1728]{2,1,0:T(8,128)(2,1)S(1)}, bf16[1,96,1728]{2,1,0:T(8,128)(2,1)S(1)}, u32[]{:S(2)}, u32[]{:S(2)}) %collective-permute-start.66) | collective-permute-done | bytes 331808 | tf_op jit(solution)/shard_map/ppermute | solution.py:39
  (466 shorter events, 222.0 us)
Async XLA Ops:
  2.4 72.5 %collective-permute-start.21 = (bf16[96,1728]{1,0:T(8,128)(2,1)S(1)}, bf16[96,1728]{1,0:T(8,128)(2,1)S(1)}, u32[]{:S(2)}, u32[]{:S(2)}) collective-permute-start(bf16[96,1728]{1,0:T(8,128)(2,1)S(1)} %pad_maximum_fusion.17), channel_id=1, source_target_pairs={{0,1},{1,2},{2,3},{3,0},{4,5},{5,6},{6,7},{7,4},{8,9},{9,10},{10,1... | collective-permute-start | bytes 995336 | tf_op jit(solution)/shard_map/ppermute | solution.py:50
  5.5 69.6 %collective-permute-start.22 = (bf16[96,1728]{1,0:T(8,128)(2,1)S(1)}, bf16[96,1728]{1,0:T(8,128)(2,1)S(1)}, u32[]{:S(2)}, u32[]{:S(2)}) collective-permute-start(bf16[96,1728]{1,0:T(8,128)(2,1)S(1)} %pad_maximum_fusion.17), channel_id=1, source_target_pairs={{0,2},{1,3},{2,0},{3,1},{4,6},{5,7},{6,4},{7,5},{8,10},{9,11},{10,... | collective-permute-start | bytes 995336 | tf_op jit(solution)/shard_map/ppermute | solution.py:50
  8.2 15.3 %collective-permute-start.9 = (f32[1152]{0:T(1024)S(1)}, f32[1152]{0:T(1024)}, u32[]{:S(2)}, u32[]{:S(2)}) collective-permute-start(f32[1152]{0:T(1024)S(1)} %concatenate.238), channel_id=1, source_target_pairs={{0,1},{1,2},{2,3},{3,0},{4,5},{5,6},{6,7},{7,4},{8,9},{9,10},{10,1... | collective-permute-start | bytes 13832 | tf_op jit(solution)/shard_map/ppermute | solution.py:50
  8.2 22.8 %collective-permute-start.10 = (f32[1152]{0:T(1024)S(1)}, f32[1152]{0:T(1024)}, u32[]{:S(2)}, u32[]{:S(2)}) collective-permute-start(f32[1152]{0:T(1024)S(1)} %concatenate.238), channel_id=1, source_target_pairs={{0,2},{1,3},{2,0},{3,1},{4,6},{5,7},{6,4},{7,5},{8,10},{9,11},{10,... | collective-permute-start | bytes 13832 | tf_op jit(solution)/shard_map/ppermute | solution.py:50
  10.1 28.7 %collective-permute-start.11 = (f32[1152]{0:T(1024)S(1)}, f32[1152]{0:T(1024)S(1)}, u32[]{:S(2)}, u32[]{:S(2)}) collective-permute-start(f32[1152]{0:T(1024)S(1)} %concatenate.238), channel_id=1, source_target_pairs={{0,3},{1,0},{2,1},{3,2},{4,7},{5,4},{6,5},{7,6},{8,11},{9,8},{10,9... | collective-permute-start | bytes 13832 | tf_op jit(solution)/shard_map/ppermute | solution.py:50
  23.5 51.9 %collective-permute-start.23 = (bf16[96,1728]{1,0:T(8,128)(2,1)S(1)}, bf16[96,1728]{1,0:T(8,128)(2,1)S(1)}, u32[]{:S(2)}, u32[]{:S(2)}) collective-permute-start(bf16[96,1728]{1,0:T(8,128)(2,1)S(1)} %pad_maximum_fusion.17), channel_id=1, source_target_pairs={{0,3},{1,0},{2,1},{3,2},{4,7},{5,4},{6,5},{7,6},{8,11},{9,8},{10,9... | collective-permute-start | bytes 995336 | tf_op jit(solution)/shard_map/ppermute | solution.py:50
  31.1 21.2 %collective-permute-start.3 = (bf16[96,576]{1,0:T(8,128)(2,1)S(1)}, bf16[96,576]{1,0:T(8,128)(2,1)}, u32[]{:S(2)}, u32[]{:S(2)}) collective-permute-start(bf16[96,576]{1,0:T(8,128)(2,1)S(1)} %pad_maximum_fusion.18), channel_id=1, source_target_pairs={{0,1},{1,2},{2,3},{3,0},{4,5},{5,6},{6,7},{7,4},{8,9},{9,10},{10,1... | collective-permute-start | bytes 331784 | tf_op jit(solution)/shard_map/ppermute | solution.py:50
  38.7 20.8 %collective-permute-start.4 = (bf16[96,576]{1,0:T(8,128)(2,1)S(1)}, bf16[96,576]{1,0:T(8,128)(2,1)}, u32[]{:S(2)}, u32[]{:S(2)}) collective-permute-start(bf16[96,576]{1,0:T(8,128)(2,1)S(1)} %pad_maximum_fusion.18), channel_id=1, source_target_pairs={{0,2},{1,3},{2,0},{3,1},{4,6},{5,7},{6,4},{7,5},{8,10},{9,11},{10,... | collective-permute-start | bytes 331784 | tf_op jit(solution)/shard_map/ppermute | solution.py:50
  60.7 12.0 %collective-permute-start.33 = (bf16[1,128,768]{2,1,0:T(8,128)(2,1)S(1)}, bf16[1,128,768]{2,1,0:T(8,128)(2,1)S(1)}, u32[]{:S(2)}, u32[]{:S(2)}) collective-permute-start(bf16[1,128,768]{2,1,0:T(8,128)(2,1)S(1)} %constant_dynamic-slice_fusion.13), channel_id=1, source_target_pairs={{0,1},{1,2},{2,3},{3,0},{4,5},{5,6},{6,7},{7,4},{8,9},{9,10},{10,1... | collective-permute-start | bytes 589832 | tf_op jit(solution)/shard_map/ppermute | solution.py:39
  75.1 18.8 %collective-permute-start.2 = (bf16[1,128,768]{2,1,0:T(8,128)(2,1)S(1)}, bf16[1,128,768]{2,1,0:T(8,128)(2,1)S(1)}, u32[]{:S(2)}, u32[]{:S(2)}) collective-permute-start(bf16[1,128,768]{2,1,0:T(8,128)(2,1)S(1)} %get-tuple-element.173), channel_id=1, source_target_pairs={{0,3},{1,0},{2,1},{3,2},{4,7},{5,4},{6,5},{7,6},{8,11},{9,8},{10,9... | collective-permute-start | bytes 589832 | tf_op jit(solution)/shard_map/ppermute | solution.py:39
  75.4 16.0 %collective-permute-start.34 = (bf16[1,128,768]{2,1,0:T(8,128)(2,1)S(1)}, bf16[1,128,768]{2,1,0:T(8,128)(2,1)S(1)}, u32[]{:S(2)}, u32[]{:S(2)}) collective-permute-start(bf16[1,128,768]{2,1,0:T(8,128)(2,1)S(1)} %get-tuple-element.169), channel_id=1, source_target_pairs={{0,2},{1,3},{2,0},{3,1},{4,6},{5,7},{6,4},{7,5},{8,10},{9,11},{10,... | collective-permute-start | bytes 589832 | tf_op jit(solution)/shard_map/ppermute | solution.py:39
  78.6 13.3 %collective-permute-start.35 = (bf16[1,128,768]{2,1,0:T(8,128)(2,1)S(1)}, bf16[1,128,768]{2,1,0:T(8,128)(2,1)S(1)}, u32[]{:S(2)}, u32[]{:S(2)}) collective-permute-start(bf16[1,128,768]{2,1,0:T(8,128)(2,1)S(1)} %get-tuple-element.167), channel_id=1, source_target_pairs={{0,3},{1,0},{2,1},{3,2},{4,7},{5,4},{6,5},{7,6},{8,11},{9,8},{10,9... | collective-permute-start | bytes 589832 | tf_op jit(solution)/shard_map/ppermute | solution.py:39
  81.6 22.7 %collective-permute-start.24 = (bf16[2,96,1728]{2,1,0:T(8,128)(2,1)S(1)}, bf16[2,96,1728]{2,1,0:T(8,128)(2,1)S(1)}, u32[]{:S(2)}, u32[]{:S(2)}) collective-permute-start(bf16[2,96,1728]{2,1,0:T(8,128)(2,1)S(1)} %get-tuple-element.155), channel_id=1, source_target_pairs={{0,8},{4,12},{8,0},{12,4},{1,9},{5,13},{9,1},{13,5},{2,10},{6,14},... | collective-permute-start | bytes 1990664 | tf_op jit(solution)/shard_map/ppermute | solution.py:26
  86.2 25.2 %collective-permute-start.27 = (bf16[2,96,1728]{2,1,0:T(8,128)(2,1)S(1)}, bf16[2,96,1728]{2,1,0:T(8,128)(2,1)S(1)}, u32[]{:S(2)}, u32[]{:S(2)}) collective-permute-start(bf16[2,96,1728]{2,1,0:T(8,128)(2,1)S(1)} %get-tuple-element.154), channel_id=1, source_target_pairs={{0,16},{16,0},{1,17},{17,1},{2,18},{18,2},{3,19},{19,3},{4,20},{20... | collective-permute-start | bytes 1990664 | tf_op jit(solution)/shard_map/ppermute | solution.py:26
  104.6 32.2 %collective-permute-start.25 = (bf16[2,2,96,1728]{3,2,0,1:T(8,128)(2,1)S(1)}, bf16[2,2,96,1728]{3,2,0,1:T(8,128)(2,1)S(1)}, u32[]{:S(2)}, u32[]{:S(2)}) collective-permute-start(bf16[2,2,96,1728]{3,2,0,1:T(8,128)(2,1)S(1)} %maximum_select_fusion.8), channel_id=1, source_target_pairs={{0,16},{16,0},{1,17},{17,1},{2,18},{18,2},{3,19},{19,3},{4,20},{20... | collective-permute-start | bytes 3981320 | tf_op jit(solution)/shard_map/ppermute | solution.py:26
  110.9 14.9 %collective-permute-start.15 = (bf16[1,512,576]{1,2,0:T(8,128)(2,1)S(1)}, bf16[1,512,576]{1,2,0:T(8,128)(2,1)S(1)}, u32[]{:S(2)}, u32[]{:S(2)}) collective-permute-start(bf16[1,512,576]{1,2,0:T(8,128)(2,1)S(1)} %constant_dynamic-slice_fusion.22), channel_id=1, source_target_pairs={{0,4},{4,8},{8,12},{12,0},{1,5},{5,9},{9,13},{13,1},{2,6},{6,10},{... | collective-permute-start | bytes 1769480 | tf_op jit(solution)/shard_map/ppermute | solution.py:39
  111.6 33.1 %collective-permute-start.28 = (bf16[2,2,96,1728]{3,2,1,0:T(8,128)(2,1)S(1)}, bf16[2,2,96,1728]{3,2,1,0:T(8,128)(2,1)S(1)}, u32[]{:S(2)}, u32[]{:S(2)}) collective-permute-start(bf16[2,2,96,1728]{3,2,1,0:T(8,128)(2,1)S(1)} %maximum_select_fusion.10), channel_id=1, source_target_pairs={{0,8},{4,12},{8,0},{12,4},{1,9},{5,13},{9,1},{13,5},{2,10},{6,14},... | collective-permute-start | bytes 3981320 | tf_op jit(solution)/shard_map/ppermute | solution.py:26
  126.0 31.5 %collective-permute-start.16 = (bf16[1,512,576]{1,2,0:T(8,128)(2,1)S(1)}, bf16[1,512,576]{1,2,0:T(8,128)(2,1)S(1)}, u32[]{:S(2)}, u32[]{:S(2)}) collective-permute-start(bf16[1,512,576]{1,2,0:T(8,128)(2,1)S(1)} %get-tuple-element.138), channel_id=1, source_target_pairs={{0,8},{4,12},{8,0},{12,4},{1,9},{5,13},{9,1},{13,5},{2,10},{6,14},... | collective-permute-start | bytes 1769480 | tf_op jit(solution)/shard_map/ppermute | solution.py:39
  138.8 89.3 %collective-permute-start.26 = (bf16[2,2,2,96,1728]{4,3,0,2,1:T(8,128)(2,1)}, bf16[2,2,2,96,1728]{4,3,0,2,1:T(8,128)(2,1)}, u32[]{:S(2)}, u32[]{:S(2)}) collective-permute-start(bf16[2,2,2,96,1728]{4,3,0,2,1:T(8,128)(2,1)} %maximum_select_fusion.2), channel_id=1, source_target_pairs={{0,4},{4,0},{8,12},{12,8},{1,5},{5,1},{9,13},{13,9},{2,6},{6,2},{1... | collective-permute-start | bytes 7962632 | tf_op jit(solution)/shard_map/ppermute | solution.py:26
  138.9 29.1 %collective-permute-start.17 = (bf16[1,512,576]{1,2,0:T(8,128)(2,1)S(1)}, bf16[1,512,576]{1,2,0:T(8,128)(2,1)S(1)}, u32[]{:S(2)}, u32[]{:S(2)}) collective-permute-start(bf16[1,512,576]{1,2,0:T(8,128)(2,1)S(1)} %get-tuple-element.137), channel_id=1, source_target_pairs={{0,12},{4,0},{8,4},{12,8},{1,13},{5,1},{9,5},{13,9},{2,14},{6,2},{... | collective-permute-start | bytes 1769480 | tf_op jit(solution)/shard_map/ppermute | solution.py:39
  146.7 86.5 %collective-permute-start.29 = (bf16[2,2,2,96,1728]{4,3,1,0,2:T(8,128)(2,1)}, bf16[2,2,2,96,1728]{4,3,1,0,2:T(8,128)(2,1)}, u32[]{:S(2)}, u32[]{:S(2)}) collective-permute-start(bf16[2,2,2,96,1728]{4,3,1,0,2:T(8,128)(2,1)} %maximum_select_fusion.4), channel_id=1, source_target_pairs={{0,4},{4,0},{8,12},{12,8},{1,5},{5,1},{9,13},{13,9},{2,6},{6,2},{1... | collective-permute-start | bytes 7962632 | tf_op jit(solution)/shard_map/ppermute | solution.py:26
  327.8 29.8 %collective-permute-start.68 = (f32[7680]{0:T(1024)S(1)}, f32[7680]{0:T(1024)S(1)}, u32[]{:S(2)}, u32[]{:S(2)}) collective-permute-start(f32[7680]{0:T(1024)S(1)} %constant_dynamic-update-slice_fusion.30), channel_id=1, source_target_pairs={{0,4},{4,0},{8,12},{12,8},{1,5},{5,1},{9,13},{13,9},{2,6},{6,2},{1... | collective-permute-start | bytes 92168 | tf_op jit(solution)/shard_map/ppermute | solution.py:26
  346.7 19.9 %collective-permute-start.36 = (bf16[1,512,192]{1,2,0:T(8,128)(2,1)S(1)}, bf16[1,512,192]{1,2,0:T(8,128)(2,1)S(1)}, u32[]{:S(2)}, u32[]{:S(2)}) collective-permute-start(bf16[1,512,192]{1,2,0:T(8,128)(2,1)S(1)} %constant_dynamic-slice_fusion.10), channel_id=1, source_target_pairs={{0,4},{4,8},{8,12},{12,0},{1,5},{5,9},{9,13},{13,1},{2,6},{6,10},{... | collective-permute-start | bytes 589832 | tf_op jit(solution)/shard_map/ppermute | solution.py:39
  348.4 81.4 %collective-permute-start.30 = (bf16[1,128,768]{2,1,0:T(8,128)(2,1)}, bf16[1,128,768]{2,1,0:T(8,128)(2,1)}, u32[]{:S(2)}, u32[]{:S(2)}) collective-permute-start(bf16[1,128,768]{2,1,0:T(8,128)(2,1)} %constant_dynamic-slice_fusion.16), channel_id=1, source_target_pairs={{0,1},{1,2},{2,3},{3,0},{4,5},{5,6},{6,7},{7,4},{8,9},{9,10},{10,1... | collective-permute-start | bytes 589832 | tf_op jit(solution)/shard_map/ppermute | solution.py:39
  373.5 56.3 %collective-permute-start.72 = (f32[7680]{0:T(1024)S(1)}, f32[7680]{0:T(1024)S(1)}, u32[]{:S(2)}, u32[]{:S(2)}) collective-permute-start(f32[7680]{0:T(1024)S(1)} %add.588), channel_id=1, source_target_pairs={{0,2},{1,3},{2,0},{3,1},{4,6},{5,7},{6,4},{7,5},{8,10},{9,11},{10,... | collective-permute-start | bytes 92168 | tf_op jit(solution)/shard_map/ppermute | solution.py:26
  422.7 25.2 %collective-permute-start.39 = (bf16[1,512,576]{1,2,0:T(8,128)(2,1)}, bf16[1,512,576]{1,2,0:T(8,128)(2,1)}, u32[]{:S(2)}, u32[]{:S(2)}) collective-permute-start(bf16[1,512,576]{1,2,0:T(8,128)(2,1)} %copy.208), channel_id=1, source_target_pairs={{0,4},{4,8},{8,12},{12,0},{1,5},{5,9},{9,13},{13,1},{2,6},{6,10},{... | collective-permute-start | bytes 1769480 | tf_op jit(solution)/shard_map/ppermute | solution.py:39
  425.1 24.2 %collective-permute-start.40 = (bf16[1,512,576]{1,2,0:T(8,128)(2,1)}, bf16[1,512,576]{1,2,0:T(8,128)(2,1)}, u32[]{:S(2)}, u32[]{:S(2)}) collective-permute-start(bf16[1,512,576]{1,2,0:T(8,128)(2,1)} %copy.209), channel_id=1, source_target_pairs={{0,8},{4,12},{8,0},{12,4},{1,9},{5,13},{9,1},{13,5},{2,10},{6,14},... | collective-permute-start | bytes 1769480 | tf_op jit(solution)/shard_map/ppermute | solution.py:39
  431.8 12.8 %collective-permute-start.31 = (bf16[1,128,768]{2,1,0:T(8,128)(2,1)}, bf16[1,128,768]{2,1,0:T(8,128)(2,1)}, u32[]{:S(2)}, u32[]{:S(2)}) collective-permute-start(bf16[1,128,768]{2,1,0:T(8,128)(2,1)} %get-tuple-element.171), channel_id=1, source_target_pairs={{0,2},{1,3},{2,0},{3,1},{4,6},{5,7},{6,4},{7,5},{8,10},{9,11},{10,... | collective-permute-start | bytes 589832 | tf_op jit(solution)/shard_map/ppermute | solution.py:39
  432.9 13.4 %collective-permute-start.32 = (bf16[1,128,768]{2,1,0:T(8,128)(2,1)}, bf16[1,128,768]{2,1,0:T(8,128)(2,1)}, u32[]{:S(2)}, u32[]{:S(2)}) collective-permute-start(bf16[1,128,768]{2,1,0:T(8,128)(2,1)} %get-tuple-element.170), channel_id=1, source_target_pairs={{0,3},{1,0},{2,1},{3,2},{4,7},{5,4},{6,5},{7,6},{8,11},{9,8},{10,9... | collective-permute-start | bytes 589832 | tf_op jit(solution)/shard_map/ppermute | solution.py:39
  435.7 17.0 %collective-permute-start.41 = (bf16[1,512,576]{1,2,0:T(8,128)(2,1)}, bf16[1,512,576]{1,2,0:T(8,128)(2,1)}, u32[]{:S(2)}, u32[]{:S(2)}) collective-permute-start(bf16[1,512,576]{1,2,0:T(8,128)(2,1)} %copy.210), channel_id=1, source_target_pairs={{0,12},{4,0},{8,4},{12,8},{1,13},{5,1},{9,5},{13,9},{2,14},{6,2},{... | collective-permute-start | bytes 1769480 | tf_op jit(solution)/shard_map/ppermute | solution.py:39
  444.6 91.4 %collective-permute-start.59 = (bf16[2,2,2,96,1728]{4,3,2,1,0:T(8,128)(2,1)}, bf16[2,2,2,96,1728]{4,3,2,1,0:T(8,128)(2,1)}, u32[]{:S(2)}, u32[]{:S(2)}) collective-permute-start(bf16[2,2,2,96,1728]{4,3,2,1,0:T(8,128)(2,1)} %select_bitcast_fusion.1), channel_id=1, source_target_pairs={{0,4},{4,0},{8,12},{12,8},{1,5},{5,1},{9,13},{13,9},{2,6},{6,2},{1... | collective-permute-start | bytes 7962632 | tf_op jit(solution)/shard_map/ppermute | solution.py:26
  464.6 13.0 %collective-permute-start.54 = (f32[4,576]{1,0:T(4,128)S(1)}, f32[4,576]{1,0:T(4,128)S(1)}, u32[]{:S(2)}, u32[]{:S(2)}) collective-permute-start(f32[4,576]{1,0:T(4,128)S(1)} %convert_reduce_fusion), channel_id=1, source_target_pairs={{0,4},{4,0},{8,12},{12,8},{1,5},{5,1},{9,13},{13,9},{2,6},{6,2},{1... | collective-permute-start | bytes 27656 | tf_op jit(solution)/shard_map/ppermute | solution.py:26
  472.6 37.8 %collective-permute-start.45 = (bf16[2,2,2,96,576]{4,3,2,1,0:T(8,128)(2,1)}, bf16[2,2,2,96,576]{4,3,2,1,0:T(8,128)(2,1)}, u32[]{:S(2)}, u32[]{:S(2)}) collective-permute-start(bf16[2,2,2,96,576]{4,3,2,1,0:T(8,128)(2,1)} %select_bitcast_fusion.4), channel_id=1, source_target_pairs={{0,4},{4,0},{8,12},{12,8},{1,5},{5,1},{9,13},{13,9},{2,6},{6,2},{1... | collective-permute-start | bytes 2654216 | tf_op jit(solution)/shard_map/ppermute | solution.py:26
  486.1 12.5 %collective-permute-start.42 = (bf16[1,128,768]{2,1,0:T(8,128)(2,1)S(1)}, bf16[1,128,768]{2,1,0:T(8,128)(2,1)S(1)}, u32[]{:S(2)}, u32[]{:S(2)}) collective-permute-start(bf16[1,128,768]{2,1,0:T(8,128)(2,1)S(1)} %constant_dynamic-slice_fusion.4), channel_id=1, source_target_pairs={{0,1},{1,2},{2,3},{3,0},{4,5},{5,6},{6,7},{7,4},{8,9},{9,10},{10,1... | collective-permute-start | bytes 589832 | tf_op jit(solution)/shard_map/ppermute | solution.py:39
  496.4 16.8 %collective-permute-start.48 = (bf16[2,2,2,96,576]{4,3,0,1,2:T(8,128)(2,1)S(1)}, bf16[2,2,2,96,576]{4,3,0,1,2:T(8,128)(2,1)S(1)}, u32[]{:S(2)}, u32[]{:S(2)}) collective-permute-start(bf16[2,2,2,96,576]{4,3,0,1,2:T(8,128)(2,1)S(1)} %select_bitcast_fusion.3), channel_id=1, source_target_pairs={{0,4},{4,0},{8,12},{12,8},{1,5},{5,1},{9,13},{13,9},{2,6},{6,2},{1... | collective-permute-start | bytes 2654216 | tf_op jit(solution)/shard_map/ppermute | solution.py:26
  498.7 11.6 %collective-permute-start.43 = (bf16[1,128,768]{2,1,0:T(8,128)(2,1)S(1)}, bf16[1,128,768]{2,1,0:T(8,128)(2,1)S(1)}, u32[]{:S(2)}, u32[]{:S(2)}) collective-permute-start(bf16[1,128,768]{2,1,0:T(8,128)(2,1)S(1)} %get-tuple-element.162), channel_id=1, source_target_pairs={{0,2},{1,3},{2,0},{3,1},{4,6},{5,7},{6,4},{7,5},{8,10},{9,11},{10,... | collective-permute-start | bytes 589832 | tf_op jit(solution)/shard_map/ppermute | solution.py:39
  510.3 30.2 %collective-permute-start.62 = (bf16[2,2,2,96,1728]{4,3,0,1,2:T(8,128)(2,1)S(1)}, bf16[2,2,2,96,1728]{4,3,0,1,2:T(8,128)(2,1)S(1)}, u32[]{:S(2)}, u32[]{:S(2)}) collective-permute-start(bf16[2,2,2,96,1728]{4,3,0,1,2:T(8,128)(2,1)S(1)} %copy-done.32), channel_id=1, source_target_pairs={{0,4},{4,0},{8,12},{12,8},{1,5},{5,1},{9,13},{13,9},{2,6},{6,2},{1... | collective-permute-start | bytes 7962632 | tf_op jit(solution)/shard_map/ppermute | solution.py:26
  512.3 13.7 %collective-permute-start.46 = (bf16[2,2,96,576]{3,2,1,0:T(8,128)(2,1)S(1)}, bf16[2,2,96,576]{3,2,1,0:T(8,128)(2,1)S(1)}, u32[]{:S(2)}, u32[]{:S(2)}) collective-permute-start(bf16[2,2,96,576]{3,2,1,0:T(8,128)(2,1)S(1)} %fusion.77), channel_id=1, source_target_pairs={{0,16},{16,0},{1,17},{17,1},{2,18},{18,2},{3,19},{19,3},{4,20},{20... | collective-permute-start | bytes 1327112 | tf_op jit(solution)/shard_map/ppermute | solution.py:26
  513.6 13.7 %collective-permute-start.49 = (bf16[2,2,96,576]{3,2,0,1:T(8,128)(2,1)S(1)}, bf16[2,2,96,576]{3,2,0,1:T(8,128)(2,1)S(1)}, u32[]{:S(2)}, u32[]{:S(2)}) collective-permute-start(bf16[2,2,96,576]{3,2,0,1:T(8,128)(2,1)S(1)} %select_bitcast_fusion.7), channel_id=1, source_target_pairs={{0,8},{4,12},{8,0},{12,4},{1,9},{5,13},{9,1},{13,5},{2,10},{6,14},... | collective-permute-start | bytes 1327112 | tf_op jit(solution)/shard_map/ppermute | solution.py:26
  535.1 12.3 %collective-permute-start.51 = (bf16[1,96,576]{2,1,0:T(8,128)(2,1)S(1)}, bf16[1,96,576]{2,1,0:T(8,128)(2,1)S(1)}, u32[]{:S(2)}, u32[]{:S(2)}) collective-permute-start(bf16[1,96,576]{2,1,0:T(8,128)(2,1)S(1)} %get-tuple-element.179), channel_id=1, source_target_pairs={{0,1},{1,2},{2,3},{3,0},{4,5},{5,6},{6,7},{7,4},{8,9},{9,10},{10,1... | collective-permute-start | bytes 331784 | tf_op jit(solution)/shard_map/ppermute | solution.py:39
  538.9 29.8 %collective-permute-start.60 = (bf16[2,2,96,1728]{3,2,1,0:T(8,128)(2,1)S(1)}, bf16[2,2,96,1728]{3,2,1,0:T(8,128)(2,1)S(1)}, u32[]{:S(2)}, u32[]{:S(2)}) collective-permute-start(bf16[2,2,96,1728]{3,2,1,0:T(8,128)(2,1)S(1)} %fusion.40), channel_id=1, source_target_pairs={{0,16},{16,0},{1,17},{17,1},{2,18},{18,2},{3,19},{19,3},{4,20},{20... | collective-permute-start | bytes 3981320 | tf_op jit(solution)/shard_map/ppermute | solution.py:26
  541.8 32.6 %collective-permute-start.63 = (bf16[2,2,96,1728]{3,2,0,1:T(8,128)(2,1)S(1)}, bf16[2,2,96,1728]{3,2,0,1:T(8,128)(2,1)S(1)}, u32[]{:S(2)}, u32[]{:S(2)}) collective-permute-start(bf16[2,2,96,1728]{3,2,0,1:T(8,128)(2,1)S(1)} %select_bitcast_fusion.2), channel_id=1, source_target_pairs={{0,8},{4,12},{8,0},{12,4},{1,9},{5,13},{9,1},{13,5},{2,10},{6,14},... | collective-permute-start | bytes 3981320 | tf_op jit(solution)/shard_map/ppermute | solution.py:26
  547.5 29.2 %collective-permute-start.53 = (bf16[1,96,576]{2,1,0:T(8,128)(2,1)S(1)}, bf16[1,96,576]{2,1,0:T(8,128)(2,1)S(1)}, u32[]{:S(2)}, u32[]{:S(2)}) collective-permute-start(bf16[1,96,576]{2,1,0:T(8,128)(2,1)S(1)} %get-tuple-element.178), channel_id=1, source_target_pairs={{0,3},{1,0},{2,1},{3,2},{4,7},{5,4},{6,5},{7,6},{8,11},{9,8},{10,9... | collective-permute-start | bytes 331784 | tf_op jit(solution)/shard_map/ppermute | solution.py:39
  569.3 17.1 %collective-permute-start.61 = (bf16[2,96,1728]{2,1,0:T(8,128)(2,1)S(1)}, bf16[2,96,1728]{2,1,0:T(8,128)(2,1)S(1)}, u32[]{:S(2)}, u32[]{:S(2)}) collective-permute-start(bf16[2,96,1728]{2,1,0:T(8,128)(2,1)S(1)} %select_bitcast_fusion.6), channel_id=1, source_target_pairs={{0,8},{4,12},{8,0},{12,4},{1,9},{5,13},{9,1},{13,5},{2,10},{6,14},... | collective-permute-start | bytes 1990664 | tf_op jit(solution)/shard_map/ppermute | solution.py:26
  575.0 11.6 %collective-permute-start.64 = (bf16[2,96,1728]{2,1,0:T(8,128)(2,1)S(1)}, bf16[2,96,1728]{2,1,0:T(8,128)(2,1)S(1)}, u32[]{:S(2)}, u32[]{:S(2)}) collective-permute-start(bf16[2,96,1728]{2,1,0:T(8,128)(2,1)S(1)} %select_bitcast_fusion.5), channel_id=1, source_target_pairs={{0,16},{16,0},{1,17},{17,1},{2,18},{18,2},{3,19},{19,3},{4,20},{20... | collective-permute-start | bytes 1990664 | tf_op jit(solution)/shard_map/ppermute | solution.py:26
  587.3 14.4 %collective-permute-start.65 = (bf16[1,96,1728]{2,1,0:T(8,128)(2,1)S(1)}, bf16[1,96,1728]{2,1,0:T(8,128)(2,1)S(1)}, u32[]{:S(2)}, u32[]{:S(2)}) collective-permute-start(bf16[1,96,1728]{2,1,0:T(8,128)(2,1)S(1)} %get-tuple-element.148), channel_id=1, source_target_pairs={{0,1},{1,2},{2,3},{3,0},{4,5},{5,6},{6,7},{7,4},{8,9},{9,10},{10,1... | collective-permute-start | bytes 995336 | tf_op jit(solution)/shard_map/ppermute | solution.py:39
  588.1 25.1 %collective-permute-start.66 = (bf16[1,96,1728]{2,1,0:T(8,128)(2,1)S(1)}, bf16[1,96,1728]{2,1,0:T(8,128)(2,1)S(1)}, u32[]{:S(2)}, u32[]{:S(2)}) collective-permute-start(bf16[1,96,1728]{2,1,0:T(8,128)(2,1)S(1)} %get-tuple-element.149), channel_id=1, source_target_pairs={{0,2},{1,3},{2,0},{3,1},{4,6},{5,7},{6,4},{7,5},{8,10},{9,11},{10,... | collective-permute-start | bytes 995336 | tf_op jit(solution)/shard_map/ppermute | solution.py:39
  594.1 19.1 %collective-permute-start.67 = (bf16[1,96,1728]{2,1,0:T(8,128)(2,1)S(1)}, bf16[1,96,1728]{2,1,0:T(8,128)(2,1)S(1)}, u32[]{:S(2)}, u32[]{:S(2)}) collective-permute-start(bf16[1,96,1728]{2,1,0:T(8,128)(2,1)S(1)} %get-tuple-element.147), channel_id=1, source_target_pairs={{0,3},{1,0},{2,1},{3,2},{4,7},{5,4},{6,5},{7,6},{8,11},{9,8},{10,9... | collective-permute-start | bytes 995336 | tf_op jit(solution)/shard_map/ppermute | solution.py:39
  (85 other events, 721.5 us)
